TPU v7x, 128 devices: a whole 4x4x4 slice. The times are simulated.
128 devices in a mesh: section: 16 (over x, y_lo, core), dp: 4 (over z), tensor: 2 (over y_hi).
Axes of the slice: x: 4, y: 4 (y_hi: 2, y_lo: 2; y = y_hi * 2 + y_lo), z: 4, core: 2. Of those that a mesh axis runs over, the one named last changes fastest.
Arguments:
- block_inputs: bfloat16 [16, 512, 3072], P('section', ('dp', 'tensor')), may hold values from -16 to 16
- qkv_weights: bfloat16 [16, 3, 3072, 3072], P('section', None, None, ('dp', 'tensor')), may hold values from -0.109375 to 0.109375
- out_weights: bfloat16 [16, 3072, 3072], P('section', ('dp', 'tensor')), may hold values from -0.109375 to 0.109375
- norm_gain: float32 [16, 3072], P('section'), may hold values from 0.25 to 1.75
- query_key_gain: float32 [16, 2, 128], P('section'), may hold values from 1.5 to 1.75
- pool_gain: float32 [16, 3072], P('section'), may hold values from 0.25 to 1.75
- class_head: bfloat16 [16, 3072, 512], P('section'), may hold values from -0.75 to 0.75
- labels: int32 [16, 2], P('section'), may hold values from 0 to 511
Outputs:
- out_rows: bfloat16 [16, 512, 3072], P('section', ('dp', 'tensor'))
- query_key_value_gradient: bfloat16 [16, 3, 3072, 3072], P('section', None, None, ('dp', 'tensor'))
- grad_out: bfloat16 [16, 3072, 3072], P('section', ('dp', 'tensor'))
- grad_head: bfloat16 [16, 3072, 512], P('section', ('dp', 'tensor'))
- losses: float32 [16, 2], P('section')
All inputs are finite; a program needn't handle non-finite values.
Results may differ from a plain program's by a relative error of at most 0.03.
Values may be sent and summed in bfloat16 or wider, within the bound.
A program may use at most 128 MiB of HBM per device.

v0:
```python
import functools
import math

import jax
import jax.numpy as jnp
from jax import lax
from jax.experimental import pallas as pl
from jax.experimental.pallas import tpu as pltpu
from jax.sharding import PartitionSpec as P

HS = 128
PATCHES = 256
EPS = 1e-06
N_DP = 4
N_T = 2
ROWS = 64
TOTAL = 512
D = 3072
F = 384
CLASSES = 512
W = 512
CHUNKS = D // W
KINDS = ("A", "B", "A", "A", "B", "A")
MESH = pl.DeviceIdType.MESH
f32 = jnp.float32
bf16 = jnp.bfloat16
VM = pl.BlockSpec(memory_space=pltpu.VMEM)
ANY = pl.BlockSpec(memory_space=pl.ANY)


def dot_nn(a, b):
    return lax.dot_general(a, b, (((1,), (0,)), ((), ())), preferred_element_type=f32)


def dot_nt(a, b):
    return lax.dot_general(a, b, (((1,), (1,)), ((), ())), preferred_element_type=f32)


def norm_last(values, gain_row):
    centered = values - jnp.mean(values, axis=-1, keepdims=True)
    inverse = lax.rsqrt(jnp.mean(centered * centered, axis=-1, keepdims=True) + EPS)
    unit_rows = centered * inverse
    return unit_rows * gain_row, unit_rows, inverse


def norm_back(grad, unit_rows, inverse, gain_row):
    scaled = grad * gain_row
    return inverse * (
        scaled
        - jnp.mean(scaled, axis=-1, keepdims=True)
        - unit_rows * jnp.mean(scaled * unit_rows, axis=-1, keepdims=True)
    )


def place():
    return lax.axis_index("dp"), lax.axis_index("tensor")


def neighbour(dz, dt):
    z, t = place()
    target = {}
    if dz:
        target["dp"] = lax.rem(z + dz + N_DP, N_DP)
    if dt:
        target["tensor"] = 1 - t
    return target


def section_at(step):
    s, n = lax.axis_index("section"), lax.axis_size("section")
    return {"section": lax.rem(s + step + n, n)}


def enter(devices):
    barrier = pltpu.get_barrier_semaphore()
    for device in devices:
        pl.semaphore_signal(barrier, inc=1, device_id=device, device_id_type=MESH)
    pl.semaphore_wait(barrier, len(devices))


def rows_of(dz, dt):
    z, t = place()
    owner = lax.rem(z + dz + N_DP, N_DP) * N_T + ((1 - t) if dt else t)
    return pl.ds(pl.multiple_of(owner * ROWS, ROWS), ROWS)


def columns(c):
    return pl.ds(c * W, W)


class Gather:
    def __init__(self, buf, send_sem, recv_sem):
        self.buf, self.send_sem, self.recv_sem = buf, send_sem, recv_sem
        self.sent = []

    def view(self, dz, dt, c):
        return self.buf.at[rows_of(dz, dt), columns(c)]

    def send(self, c, dz, dt, to_z, to_t):
        k = sum(1 for (cc, _) in self.sent if cc == c)
        slot = ((dz - to_z) % N_DP) * 2 + (dt ^ to_t)
        part = self.view(dz, dt, c)
        copy = pltpu.make_async_remote_copy(
            src_ref=part,
            dst_ref=part,
            send_sem=self.send_sem.at[c, k],
            recv_sem=self.recv_sem.at[c, slot],
            device_id=neighbour(to_z, to_t),
            device_id_type=MESH,
        )
        copy.start()
        self.sent.append((c, copy))

    def recv(self, c, dz, dt):
        part = self.view(dz, dt, c)
        pltpu.make_async_remote_copy(
            src_ref=part,
            dst_ref=part,
            send_sem=self.send_sem.at[c, 0],
            recv_sem=self.recv_sem.at[c, (dz % N_DP) * 2 + dt],
            device_id=neighbour(1, 0),
            device_id_type=MESH,
        ).wait_recv()

    def begin(self, c):
        if KINDS[c] == "A":
            self.send(c, 0, 0, 0, 1)
            self.send(c, 0, 0, 1, 0)
            self.send(c, 0, 0, -1, 0)
        else:
            self.send(c, 0, 0, 1, 0)
            self.send(c, 0, 0, -1, 0)
            self.send(c, 0, 0, 0, 1)

    def first(self, c):
        if KINDS[c] == "A":
            self.recv(c, 0, 1)
            self.send(c, 0, 1, 1, 0)
            self.send(c, 0, 1, -1, 0)
            self.recv(c, -1, 0)
            self.send(c, -1, 0, 1, 0)
        else:
            way = 1 if c % 2 else -1
            self.recv(c, -way, 0)
            self.send(c, -way, 0, way, 0)
            self.send(c, -way, 0, 0, 1)
            self.recv(c, way, 0)
            self.send(c, way, 0, 0, 1)

    def second(self, c):
        if KINDS[c] == "A":
            self.recv(c, 1, 1)
            self.send(c, 1, 1, -1, 0)
        else:
            self.recv(c, 2, 0)
            self.send(c, 2, 0, 0, 1)

    def third(self, c):
        if KINDS[c] == "A":
            rest = ((1, 0), (-1, 1), (2, 0), (2, 1))
        else:
            rest = ((0, 1), (-1, 1), (1, 1), (2, 1))
        for dz, dt in rest:
            self.recv(c, dz, dt)

    def run(self, compute):
        for c in range(CHUNKS):
            self.begin(c)
        for i in range(CHUNKS + 2):
            if i < CHUNKS:
                self.first(i)
            if 0 <= i - 1 < CHUNKS:
                self.second(i - 1)
            if i >= 2:
                self.third(i - 2)
                compute(i - 2)

    def finish(self):
        for _, copy in self.sent:
            copy.wait_send()


RING = ((1, 0), (-1, 0), (0, 1))


class Scatter:
    def __init__(self, part, land, send_sem, recv_sem):
        self.part, self.land = part, land
        self.send_sem, self.recv_sem = send_sem, recv_sem
        self.sent = []

    def view(self, dz, dt, c):
        return self.part.at[rows_of(dz, dt), columns(c)]

    def send(self, c, dz, dt, to_z, to_t, slot):
        copy = pltpu.make_async_remote_copy(
            src_ref=self.view(dz, dt, c),
            dst_ref=self.land.at[c, slot],
            send_sem=self.send_sem.at[c, slot],
            recv_sem=self.recv_sem.at[c, slot],
            device_id=neighbour(to_z, to_t),
            device_id_type=MESH,
        )
        copy.start()
        self.sent.append(copy)

    def recv(self, c, slot):
        pltpu.make_async_remote_copy(
            src_ref=self.view(0, 0, c),
            dst_ref=self.land.at[c, slot],
            send_sem=self.send_sem.at[c, slot],
            recv_sem=self.recv_sem.at[c, slot],
            device_id=neighbour(1, 0),
            device_id_type=MESH,
        ).wait_recv()
        return self.land[c, slot].astype(f32)

    def value(self, dz, dt, c):
        return self.part[rows_of(dz, dt), columns(c)].astype(f32)

    def put(self, dz, dt, c, value):
        self.part[rows_of(dz, dt), columns(c)] = value.astype(bf16)

    def begin(self, c):
        if KINDS[c] == "A":
            self.send(c, 2, 0, 1, 0, 0)
            self.send(c, 2, 1, -1, 0, 1)
            self.send(c, -1, 0, -1, 0, 2)
            self.send(c, 1, 1, 1, 0, 3)
        else:
            self.send(c, 2, 1, 0, 1, 0)
            self.send(c, 1, 1, 0, 1, 1)
            self.send(c, -1, 1, 0, 1, 2)
            self.send(c, 0, 1, 0, 1, 3)

    def first(self, c):
        if KINDS[c] == "A":
            self.put(1, 0, c, self.value(1, 0, c) + self.recv(c, 0))
            self.send(c, 1, 0, 1, 0, 4)
            self.put(-1, 1, c, self.value(-1, 1, c) + self.recv(c, 1))
            self.send(c, -1, 1, -1, 0, 5)
        else:
            way = 1 if c % 2 else -1
            self.put(2, 0, c, self.value(2, 0, c) + self.recv(c, 0))
            self.send(c, 2, 0, way, 0, 4)
            other = 2 if way == 1 else 1
            self.put(-way, 0, c, self.value(-way, 0, c) + self.recv(c, other))
            self.send(c, -way, 0, -way, 0, 5)

    def second(self, c):
        if KINDS[c] == "A":
            total = self.value(0, 1, c) + self.recv(c, 3) + self.recv(c, 5)
            self.put(0, 1, c, total)
            self.send(c, 0, 1, 0, 1, 6)
        else:
            way = 1 if c % 2 else -1
            other = 1 if way == 1 else 2
            total = self.value(way, 0, c) + self.recv(c, other) + self.recv(c, 4)
            self.put(way, 0, c, total)
            self.send(c, way, 0, way, 0, 6)

    def third(self, c):
        rest = (2, 4, 6) if KINDS[c] == "A" else (3, 5, 6)
        total = self.value(0, 0, c)
        for slot in rest:
            total = total + self.recv(c, slot)
        return total

    def run(self, compute, done):
        for i in range(CHUNKS + 3):
            if i < CHUNKS:
                compute(i)
                self.begin(i)
            if 0 <= i - 1 < CHUNKS:
                self.first(i - 1)
            if 0 <= i - 2 < CHUNKS:
                self.second(i - 2)
            if 0 <= i - 3:
                done(i - 3, self.third(i - 3))

    def finish(self):
        for copy in self.sent:
            copy.wait_send()


def project_kernel(
    rows_ref, gain_ref, w_hbm, proj_ref, turned_ref, buf, wbuf, wsem, send_sem, recv_sem
):
    load = pltpu.make_async_copy(w_hbm, wbuf, wsem)
    load.start()
    normed, _, _ = norm_last(rows_ref[...].astype(f32), gain_ref[...])
    buf[rows_of(0, 0), :] = normed.astype(bf16)
    enter([neighbour(*way) for way in RING])
    gather = Gather(buf, send_sem, recv_sem)

    def compute(c):
        if c == 0:
            load.wait()

        def tile(r, carry):
            rows = pl.ds(pl.multiple_of(r * 256, 256), 256)
            block = buf[rows, columns(c)]
            for t in range(3):
                value = dot_nn(block, wbuf[t, columns(c), :])
                cols = pl.ds(t * F, F)
                if c == 0:
                    proj_ref[rows, cols] = value
                else:
                    proj_ref[rows, cols] += value
            turned_ref[columns(c), rows] = block.T
            return carry

        lax.fori_loop(0, TOTAL // 256, tile, 0)

    gather.run(compute)
    gather.finish()


def params(collective_id=None, limit=60 * 1024 * 1024):
    if collective_id is None:
        return pltpu.CompilerParams(vmem_limit_bytes=limit)
    return pltpu.CompilerParams(
        collective_id=collective_id, has_side_effects=True, vmem_limit_bytes=limit
    )


def ring_sems():
    return [pltpu.SemaphoreType.DMA((CHUNKS, 8)), pltpu.SemaphoreType.DMA((CHUNKS, 8))]


def project(rows, gain_row, qkv_local, collective_id):
    return pl.pallas_call(
        project_kernel,
        out_shape=(
            jax.ShapeDtypeStruct((TOTAL, 3 * F), f32),
            jax.ShapeDtypeStruct((D, TOTAL), bf16),
        ),
        in_specs=[VM, VM, ANY],
        out_specs=(VM, VM),
        scratch_shapes=[
            pltpu.VMEM((TOTAL, D), bf16),
            pltpu.VMEM((3, D, F), bf16),
            pltpu.SemaphoreType.DMA,
        ]
        + ring_sems(),
        compiler_params=params(collective_id),
        name=f"project_{collective_id}",
    )(rows, gain_row, qkv_local)


def head_state(q_ref, k_ref, v_ref, pair_ref):
    q_normed, q_unit, q_inv = norm_last(q_ref[...], pair_ref[0:1, :])
    k_normed, k_unit, k_inv = norm_last(k_ref[...], pair_ref[1:2, :])
    q_half, k_half = q_normed.astype(bf16), k_normed.astype(bf16)
    v_half = v_ref[...].astype(bf16)
    exponent = jnp.exp(dot_nt(q_half, k_half) * (1.0 / math.sqrt(HS)))
    probs = exponent * (1.0 / jnp.sum(exponent, axis=-1, keepdims=True))
    return q_unit, q_inv, k_unit, k_inv, q_half, k_half, v_half, probs


def attend_kernel(q_ref, k_ref, v_ref, pair_ref, att_ref, turned_ref):
    v_half, probs = head_state(q_ref, k_ref, v_ref, pair_ref)[-2:]
    mixed = dot_nn(probs.astype(bf16), v_half)
    att_ref[...] = mixed.astype(bf16)
    turned_ref[...] = mixed.T.astype(bf16)


def qkv_specs():
    return [
        pl.BlockSpec((PATCHES, HS), lambda i, h, t=t: (i, 3 * t + h)) for t in range(3)
    ] + [pl.BlockSpec((2, HS), lambda i, h: (0, 0))]


def attend(projected, gain_pair):
    return pl.pallas_call(
        attend_kernel,
        grid=(2, 3),
        out_shape=(
            jax.ShapeDtypeStruct((TOTAL, F), bf16),
            jax.ShapeDtypeStruct((F, TOTAL), bf16),
        ),
        in_specs=qkv_specs(),
        out_specs=(
            pl.BlockSpec((PATCHES, HS), lambda i, h: (i, h)),
            pl.BlockSpec((HS, PATCHES), lambda i, h: (h, i)),
        ),
        compiler_params=params(),
        name="attend",
    )(projected, projected, projected, gain_pair)


def attend_back_kernel(shared, q_ref, k_ref, v_ref, pair_ref, grad_ref, out_ref):
    q_unit, q_inv, k_unit, k_inv, q_half, k_half, v_half, probs = head_state(
        q_ref, k_ref, v_ref, pair_ref
    )
    if shared:
        row = grad_ref[pl.ds(pl.program_id(0), 1), :]
        mixed = jnp.broadcast_to(row, (PATCHES, HS)).astype(bf16)
    else:
        mixed = grad_ref[...].astype(bf16)
    grad_probs = dot_nt(mixed, v_half)
    probs_t = probs.T.astype(bf16)
    grad_value = dot_nn(probs_t, mixed)
    grad_scores = probs * (grad_probs - jnp.sum(probs * grad_probs, axis=-1, keepdims=True))
    scaled = grad_scores * (1.0 / math.sqrt(HS))
    score_half = scaled.astype(bf16)
    grad_query = dot_nn(score_half, k_half)
    grad_key = dot_nn(scaled.T.astype(bf16), q_half)
    out_ref[0] = norm_back(grad_query, q_unit, q_inv, pair_ref[0:1, :]).astype(bf16)
    out_ref[1] = norm_back(grad_key, k_unit, k_inv, pair_ref[1:2, :]).astype(bf16)
    out_ref[2] = grad_value.astype(bf16)


def attend_back(projected, gain_pair, grad, shared):
    if shared:
        grad_spec = pl.BlockSpec((8, HS), lambda i, h: (0, h))
    else:
        grad_spec = pl.BlockSpec((PATCHES, HS), lambda i, h: (i, h))
    return pl.pallas_call(
        functools.partial(attend_back_kernel, shared),
        grid=(2, 3),
        out_shape=jax.ShapeDtypeStruct((3, TOTAL, F), bf16),
        in_specs=qkv_specs() + [grad_spec],
        out_specs=pl.BlockSpec((3, PATCHES, HS), lambda i, h: (0, i, h)),
        compiler_params=params(),
        name="attend_back",
    )(projected, projected, projected, gain_pair, grad)


def out_kernel(
    att_ref,
    w_ref,
    rows_ref,
    out_ref,
    margin_ref,
    part,
    land,
    next_rows,
    send_sem,
    recv_sem,
    step_send,
    step_recv,
):
    enter(
        [neighbour(*way) for way in RING] + [section_at(1), section_at(-1)]
    )
    scatter = Scatter(part, land, send_sem, recv_sem)
    hops = []

    def compute(c):
        def tile(r, carry):
            rows = pl.ds(pl.multiple_of(r * 256, 256), 256)
            part[rows, columns(c)] = dot_nn(att_ref[rows, :], w_ref[:, columns(c)]).astype(bf16)
            return carry

        lax.fori_loop(0, TOTAL // 256, tile, 0)

    def done(c, total):
        out_ref[:, columns(c)] = (rows_ref[:, columns(c)].astype(f32) + total).astype(bf16)
        copy = pltpu.make_async_remote_copy(
            src_ref=out_ref.at[:, columns(c)],
            dst_ref=next_rows.at[:, columns(c)],
            send_sem=step_send.at[c],
            recv_sem=step_recv.at[c],
            device_id=section_at(1),
            device_id_type=MESH,
        )
        copy.start()
        hops.append(copy)

    scatter.run(compute, done)
    for copy in hops:
        copy.wait_recv()
    first = lax.axis_index("section") == 0
    margin_ref[...] = jnp.where(first, rows_ref[...], next_rows[...])
    scatter.finish()
    for copy in hops:
        copy.wait_send()


def land_scratch():
    return [pltpu.VMEM((TOTAL, D), bf16), pltpu.VMEM((CHUNKS, 7, ROWS, W), bf16)]


def out_rows(attention, out_local, rows, collective_id):
    return pl.pallas_call(
        out_kernel,
        out_shape=(jax.ShapeDtypeStruct((ROWS, D), bf16), jax.ShapeDtypeStruct((ROWS, D), bf16)),
        in_specs=[VM, VM, VM],
        out_specs=(VM, VM),
        scratch_shapes=land_scratch()
        + [pltpu.VMEM((ROWS, D), bf16)]
        + ring_sems()
        + [pltpu.SemaphoreType.DMA((CHUNKS,)), pltpu.SemaphoreType.DMA((CHUNKS,))],
        compiler_params=params(collective_id),
        name="out_rows",
    )(attention, out_local, rows)


PEERS = tuple((dz, dt) for dz in range(N_DP) for dt in range(N_T) if dz or dt)
PACK = D // 4


def pack_rows(ref, value):
    for i in range(2):
        for q in range(4):
            ref[i * 4 + q : i * 4 + q + 1, :] = value[i : i + 1, q * PACK : (q + 1) * PACK]


def head_kernel(
    att_ref,
    w_ref,
    rows_ref,
    label_ref,
    pool_ref,
    head_hbm,
    loss_ref,
    head_grad_ref,
    image_ref,
    per_image_ref,
    sums_ref,
    head,
    stage,
    land,
    pooled_ref,
    half_ref,
    head_sem,
    send_sem,
    recv_sem,
):
    load = pltpu.make_async_copy(head_hbm, head, head_sem)
    load.start()
    row_id = lax.broadcasted_iota(jnp.int32, (8, 1), 0)
    sums_ref[...] = jnp.zeros_like(sums_ref)
    for i in range(2):
        block = att_ref[i * PATCHES : (i + 1) * PATCHES, :].astype(f32)
        sums_ref[i : i + 1, :] = jnp.sum(block, axis=0, keepdims=True)
    sums = sums_ref[...]
    hi = sums.astype(bf16)
    rest = sums - hi.astype(f32)
    mid = rest.astype(bf16)
    low = (rest - mid.astype(f32)).astype(bf16)
    w_out = w_ref[...]
    partial_rows = dot_nn(hi, w_out) + dot_nn(mid, w_out) + dot_nn(low, w_out)
    own = jnp.sum(rows_ref[...].astype(f32), axis=0, keepdims=True)
    image = lax.axis_index("dp") // (N_DP // 2)
    partial_rows = partial_rows + jnp.where(row_id == image, own, 0.0)
    pack_rows(stage, partial_rows)
    enter([neighbour(*way) for way in PEERS])
    copies = []
    for k, way in enumerate(PEERS):
        copy = pltpu.make_async_remote_copy(
            src_ref=stage,
            dst_ref=land.at[k],
            send_sem=send_sem.at[k],
            recv_sem=recv_sem.at[k],
            device_id=neighbour(*way),
            device_id_type=MESH,
        )
        copy.start()
        copies.append(copy)
    load.wait()
    total = stage[...]
    for k, copy in enumerate(copies):
        copy.wait_recv()
        total = total + land[k]
    pooled_ref[...] = jnp.zeros_like(pooled_ref)
    for i in range(2):
        for q in range(4):
            pooled_ref[i : i + 1, q * PACK : (q + 1) * PACK] = total[i * 4 + q : i * 4 + q + 1, :]
    pooled = pooled_ref[...] / PATCHES
    gain = pool_ref[...]
    normed, unit_rows, inverse = norm_last(pooled, gain)
    half = normed.astype(bf16)
    half_ref[...] = half.astype(f32)
    logits = dot_nn(half, head[...])
    targets = (label_ref[...] == lax.broadcasted_iota(jnp.int32, (8, CLASSES), 1)).astype(f32)
    soft = jnp.maximum(logits, 0.0) + jnp.log1p(jnp.exp(-jnp.abs(logits)))
    loss = jnp.mean(soft - targets * logits, axis=-1, keepdims=True)
    loss_ref[...] = jnp.broadcast_to(loss, loss_ref.shape)
    grad_logits = (jax.nn.sigmoid(logits) - targets) / 2
    grad_logits = jnp.where(row_id < 2, grad_logits, 0.0).astype(bf16)
    z, t = place()
    width = D // (N_DP * N_T)
    start = pl.multiple_of((z * N_T + t) * width, width)
    mine = half_ref[:, pl.ds(start, width)]
    head_grad_ref[...] = dot_nn(mine.T.astype(bf16), grad_logits).astype(bf16)
    grad_pooled = norm_back(dot_nt(grad_logits, head[...]), unit_rows, inverse, gain)
    grad_image = grad_pooled / PATCHES
    image_ref[...] = jnp.where(row_id < 2, grad_image, 0.0)
    per_image_ref[...] = dot_nt(grad_image.astype(bf16), w_out)
    for copy in copies:
        copy.wait_send()


def classify(attention, out_local, margin_rows, labels8, pool_row, head_local, collective_id):
    return pl.pallas_call(
        head_kernel,
        out_shape=(
            jax.ShapeDtypeStruct((8, 128), f32),
            jax.ShapeDtypeStruct((F, CLASSES), bf16),
            jax.ShapeDtypeStruct((8, D), f32),
            jax.ShapeDtypeStruct((8, F), f32),
            jax.ShapeDtypeStruct((8, F), f32),
        ),
        in_specs=[VM, VM, VM, VM, VM, ANY],
        out_specs=(VM,) * 5,
        scratch_shapes=[
            pltpu.VMEM((D, CLASSES), bf16),
            pltpu.VMEM((8, PACK), f32),
            pltpu.VMEM((len(PEERS), 8, PACK), f32),
            pltpu.VMEM((8, D), f32),
            pltpu.VMEM((8, D), f32),
            pltpu.SemaphoreType.DMA,
            pltpu.SemaphoreType.DMA((len(PEERS),)),
            pltpu.SemaphoreType.DMA((len(PEERS),)),
        ],
        compiler_params=params(collective_id),
        name="classify",
    )(attention, out_local, margin_rows, labels8, pool_row, head_local)


def input_grad_kernel(
    grad_ref,
    w_hbm,
    rows_ref,
    gain_ref,
    image_ref,
    back_ref,
    part,
    land,
    wbuf,
    total_ref,
    mine,
    came,
    wsem,
    send_sem,
    recv_sem,
    step_send,
    step_recv,
):
    loads = []
    for c in range(CHUNKS):
        load = pltpu.make_async_copy(
            w_hbm.at[:, columns(c), :], wbuf.at[:, columns(c), :], wsem.at[c]
        )
        load.start()
        loads.append(load)
    enter([neighbour(*way) for way in RING] + [section_at(1), section_at(-1)])
    scatter = Scatter(part, land, send_sem, recv_sem)

    def compute(c):
        loads[c].wait()

        def tile(r, carry):
            rows = pl.ds(pl.multiple_of(r * 256, 256), 256)
            value = dot_nt(grad_ref[0, rows, :], wbuf[0, columns(c), :])
            value = value + dot_nt(grad_ref[1, rows, :], wbuf[1, columns(c), :])
            value = value + dot_nt(grad_ref[2, rows, :], wbuf[2, columns(c), :])
            part[rows, columns(c)] = value.astype(bf16)
            return carry

        lax.fori_loop(0, TOTAL // 256, tile, 0)

    def done(c, total):
        total_ref[:, columns(c)] = total

    scatter.run(compute, done)
    gain = gain_ref[...]
    _, unit_rows, inverse = norm_last(rows_ref[...].astype(f32), gain)
    image = lax.axis_index("dp") // (N_DP // 2)
    residual = jnp.where(image == 0, image_ref[0:1, :], image_ref[1:2, :])
    grad = residual + norm_back(total_ref[...], unit_rows, inverse, gain)
    mine[...] = grad.astype(bf16)
    copies = []
    for c in range(2):
        part_columns = pl.ds(c * (D // 2), D // 2)
        copy = pltpu.make_async_remote_copy(
            src_ref=mine.at[:, part_columns],
            dst_ref=came.at[:, part_columns],
            send_sem=step_send.at[c],
            recv_sem=step_recv.at[c],
            device_id=section_at(-1),
            device_id_type=MESH,
        )
        copy.start()
        copies.append(copy)
    scatter.finish()
    for copy in copies:
        copy.wait_recv()
    last = lax.axis_index("section") == lax.axis_size("section") - 1
    back_ref[...] = jnp.where(last, jnp.zeros_like(came), came[...])
    for copy in copies:
        copy.wait_send()


def input_grads(projection_gradient, qkv_local, margin_rows, gain_row, grad_image, collective_id):
    return pl.pallas_call(
        input_grad_kernel,
        out_shape=jax.ShapeDtypeStruct((ROWS, D), bf16),
        in_specs=[VM, ANY, VM, VM, VM],
        out_specs=VM,
        scratch_shapes=land_scratch()
        + [
            pltpu.VMEM((3, D, F), bf16),
            pltpu.VMEM((ROWS, D), f32),
            pltpu.VMEM((ROWS, D), bf16),
            pltpu.VMEM((ROWS, D), bf16),
            pltpu.SemaphoreType.DMA((CHUNKS,)),
        ]
        + ring_sems()
        + [pltpu.SemaphoreType.DMA((2,)), pltpu.SemaphoreType.DMA((2,))],
        compiler_params=params(collective_id),
        name="input_grads",
    )(projection_gradient, qkv_local, margin_rows, gain_row, grad_image)


def cotangent_kernel(
    rows_ref,
    w_ref,
    turned_ref,
    sums_ref,
    image_ref,
    margin_turned_ref,
    margin_grad_ref,
    grad_att_ref,
    grad_out_ref,
    margin_part_ref,
    buf,
    send_sem,
    recv_sem,
):
    buf[rows_of(0, 0), :] = rows_ref[...]
    enter([neighbour(*way) for way in RING])
    gather = Gather(buf, send_sem, recv_sem)
    sums = sums_ref[...]
    hi = sums.T.astype(bf16)
    low = (sums.T - hi.astype(f32)).astype(bf16)

    def compute(c):
        def tile(r, carry):
            rows = pl.ds(pl.multiple_of(r * 256, 256), 256)
            value = dot_nt(buf[rows, columns(c)], w_ref[:, columns(c)])
            if c == 0:
                grad_att_ref[rows, :] = value
            else:
                grad_att_ref[rows, :] += value
            return carry

        lax.fori_loop(0, TOTAL // 256, tile, 0)
        shared = image_ref[:, columns(c)].astype(bf16)
        value = dot_nn(turned_ref[...], buf[:, columns(c)])
        value = value + dot_nn(hi, shared) + dot_nn(low, shared)
        grad_out_ref[:, columns(c)] = value.astype(bf16)

        def margin_tile(r, carry):
            rows = pl.ds(pl.multiple_of(c * W + r * 256, 256), 256)
            for t in range(3):
                margin_part_ref[t, rows, :] = dot_nn(
                    margin_turned_ref[rows, :], margin_grad_ref[t]
                ).astype(bf16)
            return carry

        lax.fori_loop(0, W // 256, margin_tile, 0)

    gather.run(compute)
    gather.finish()


def cotangents(returned, out_local, turned, sums, grad_image, margin_turned, margin_grad, collective_id):
    return pl.pallas_call(
        cotangent_kernel,
        out_shape=(
            jax.ShapeDtypeStruct((TOTAL, F), f32),
            jax.ShapeDtypeStruct((F, D), bf16),
            jax.ShapeDtypeStruct((3, D, F), bf16),
        ),
        in_specs=[VM] * 7,
        out_specs=(VM,) * 3,
        scratch_shapes=[pltpu.VMEM((TOTAL, D), bf16)] + ring_sems(),
        compiler_params=params(collective_id),
        name="cotangents",
    )(returned, out_local, turned, sums, grad_image, margin_turned, margin_grad)


def weight_kernel(turned_ref, grad_ref, part_ref, out_ref):
    value = dot_nn(turned_ref[...], grad_ref[0]) + part_ref[0].astype(f32)
    out_ref[0] = value.astype(bf16)


def weight_grads(turned, projection_gradient, margin_part):
    tall = 768
    return pl.pallas_call(
        weight_kernel,
        grid=(D // tall, 3),
        out_shape=jax.ShapeDtypeStruct((3, D, F), bf16),
        in_specs=[
            pl.BlockSpec((tall, TOTAL), lambda r, t: (r, 0)),
            pl.BlockSpec((1, TOTAL, F), lambda r, t: (t, 0, 0)),
            pl.BlockSpec((1, tall, F), lambda r, t: (t, r, 0)),
        ],
        out_specs=pl.BlockSpec((1, tall, F), lambda r, t: (t, r, 0)),
        compiler_params=params(),
        name="weight_grads",
    )(turned, projection_gradient, margin_part)


def on_device(
    block_inputs, qkv_weights, out_weights, norm_gain, query_key_gain, pool_gain, class_head, labels
):
    rows_in, qkv_local, out_local = block_inputs[0], qkv_weights[0], out_weights[0]
    gain_pair = query_key_gain[0]
    labels8 = jnp.broadcast_to(jnp.pad(labels[0], (0, 6))[:, None], (8, CLASSES))

    projected_own, turned_own = project(rows_in, norm_gain, qkv_local, 0)
    attention_own, attention_turned = attend(projected_own, gain_pair)
    out_own, margin_rows = out_rows(attention_own, out_local, rows_in, 1)

    projected, turned = project(margin_rows, norm_gain, qkv_local, 2)
    attention, _ = attend(projected, gain_pair)
    losses, grad_head, grad_image, per_image, sums = classify(
        attention, out_local, margin_rows, labels8, pool_gain, class_head[0], 3
    )
    margin_grad = attend_back(projected, gain_pair, per_image, True)
    returned = input_grads(margin_grad, qkv_local, margin_rows, norm_gain, grad_image, 4)

    grad_attention, grad_out, margin_part = cotangents(
        returned, out_local, attention_turned, sums, grad_image, turned, margin_grad, 5
    )
    own_grad = attend_back(projected_own, gain_pair, grad_attention, False)
    qkv_grad = weight_grads(turned_own, own_grad, margin_part)
    return (
        out_own[None],
        qkv_grad[None],
        grad_out[None],
        grad_head[None],
        losses[:2, 0][None],
    )


def solution(mesh):
    in_specs = (
        P("section", ("dp", "tensor"), None),
        P("section", None, None, ("dp", "tensor")),
        P("section", ("dp", "tensor"), None),
        P("section", None),
        P("section", None, None),
        P("section", None),
        P("section", None, None),
        P("section", None),
    )
    out_specs = (
        P("section", ("dp", "tensor"), None),
        P("section", None, None, ("dp", "tensor")),
        P("section", ("dp", "tensor"), None),
        P("section", ("dp", "tensor"), None),
        P("section", None),
    )
    return jax.shard_map(
        on_device, mesh=mesh, in_specs=in_specs, out_specs=out_specs, check_vma=False
    )
```

profile of v0, /device:TPU:1, one launch (start us, length us, event | category | flops | bytes accessed | tf_op | source)
XLA Modules:
  0.0 271.3 jit_solution(4668183925995342132)
XLA Ops:
  0.6 0.7 pad.4
  1.3 0.7 broadcast_in_dim.19.label_ref
  2.0 37.1 %project_0.1 = (f32[512,1152]{1,0:T(8,128)}, bf16[3072,512]{1,0:T(8,128)(2,1)}) custom-call(bf16[64,3072]{1,0:T(8,128)(2,1)} %bitcast.20, f32[1,3072]{1,0:T(1,128)} %gain_ref.5, bf16[3,3072,384]{2,1,0:T(8,128)(2,1)} %bitcast.11), custom_call_target="tpu_custom_call" | custom-call | tf_op jit(solution)/shard_map/project_0/pallas_call | solution.py:332
  39.1 6.8 %attend.2 = (bf16[512,384]{1,0:T(8,128)(2,1)}, bf16[384,512]{1,0:T(8,128)(2,1)}) custom-call(f32[512,1152]{1,0:T(8,128)} %get-tuple-element.22.q_ref.k_ref.v_ref, f32[512,1152]{1,0:T(8,128)} %get-tuple-element.22.q_ref.k_ref.v_ref, f32[512,1152]{1,0:T(8,128)} %get-tuple-element.22.q_ref.k_ref.v_ref, f32[2,128]{1,0:T(2,128)} %bitcast.24), custom_call_target="tpu_custom_call" | custom-call | tf_op jit(solution)/shard_map/attend/pallas_call | solution.py:375
  45.8 42.7 %out_rows.1 = (bf16[64,3072]{1,0:T(8,128)(2,1)}, bf16[64,3072]{1,0:T(8,128)(2,1)}) custom-call(bf16[512,384]{1,0:T(8,128)(2,1)} %get-tuple-element.23.att_ref, bf16[384,3072]{1,0:T(8,128)(2,1)} %bitcast.14, bf16[64,3072]{1,0:T(8,128)(2,1)} %bitcast.21), custom_call_target="tpu_custom_call" | custom-call | tf_op jit(solution)/shard_map/out_rows/pallas_call | solution.py:486
  88.5 32.5 %project_2.1 = (f32[512,1152]{1,0:T(8,128)}, bf16[3072,512]{1,0:T(8,128)(2,1)}) custom-call(bf16[64,3072]{1,0:T(8,128)(2,1)} %get-tuple-element.26.rows_ref, f32[1,3072]{1,0:T(1,128)} %gain_ref.5, bf16[3,3072,384]{2,1,0:T(8,128)(2,1)} %bitcast.12), custom_call_target="tpu_custom_call" | custom-call | tf_op jit(solution)/shard_map/project_2/pallas_call | solution.py:332
  121.0 6.8 %attend.3 = (bf16[512,384]{1,0:T(8,128)(2,1)}, bf16[384,512]{1,0:T(8,128)(2,1)}) custom-call(f32[512,1152]{1,0:T(8,128)} %get-tuple-element.27.q_ref.k_ref.v_ref, f32[512,1152]{1,0:T(8,128)} %get-tuple-element.27.q_ref.k_ref.v_ref, f32[512,1152]{1,0:T(8,128)} %get-tuple-element.27.q_ref.k_ref.v_ref, f32[2,128]{1,0:T(2,128)} %bitcast.25), custom_call_target="tpu_custom_call" | custom-call | tf_op jit(solution)/shard_map/attend/pallas_call | solution.py:375
  127.7 15.0 %classify.1 = (f32[8,128]{1,0:T(8,128)}, bf16[384,512]{1,0:T(8,128)(2,1)}, f32[8,3072]{1,0:T(8,128)}, f32[8,384]{1,0:T(8,128)}, f32[8,384]{1,0:T(8,128)}) custom-call(bf16[512,384]{1,0:T(8,128)(2,1)} %get-tuple-element.28.att_ref, bf16[384,3072]{1,0:T(8,128)(2,1)} %bitcast.15, bf16[64,3072]{1,0:T(8,128)(2,1)} %get-tuple-element.26.rows_ref, ...), custom_call_target="tpu_custom_call" | custom-call | tf_op jit(solution)/shard_map/classify/pallas_call | solution.py:597
  142.8 7.9 %attend_back.2.grad_ref.margin_grad_ref = bf16[3,512,384]{2,1,0:T(8,128)(2,1)} custom-call(f32[512,1152]{1,0:T(8,128)} %get-tuple-element.27.q_ref.k_ref.v_ref, f32[512,1152]{1,0:T(8,128)} %get-tuple-element.27.q_ref.k_ref.v_ref, f32[512,1152]{1,0:T(8,128)} %get-tuple-element.27.q_ref.k_ref.v_ref, f32[2,128]{1,0:T(2,128)} %bitcast.26, ...), custom_call_target="tpu_custom_call" | custom-call | tf_op jit(solution)/shard_map/attend_back/pallas_call | solution.py:419
  150.7 50.9 %input_grads.1.rows_ref = bf16[64,3072]{1,0:T(8,128)(2,1)} custom-call(bf16[3,512,384]{2,1,0:T(8,128)(2,1)} %attend_back.2.grad_ref.margin_grad_ref, bf16[3,3072,384]{2,1,0:T(8,128)(2,1)} %bitcast.13, bf16[64,3072]{1,0:T(8,128)(2,1)} %get-tuple-element.26.rows_ref, f32[1,3072]{1,0:T(1,128)} %gain_ref.5, f32[8,3072]{1,0:T(8,128)} %get-tuple-element.30.image_ref), custom_call_target="tpu_custom_call" | custom-call | tf_op jit(solution)/shard_map/input_grads/pallas_call | solution.py:698
  201.6 1.3 slice_reduce_fusion
  202.9 43.0 %cotangents.1 = (f32[512,384]{1,0:T(8,128)}, bf16[384,3072]{1,0:T(8,128)(2,1)}, bf16[3,3072,384]{2,1,0:T(8,128)(2,1)}) custom-call(bf16[64,3072]{1,0:T(8,128)(2,1)} %input_grads.1.rows_ref, bf16[384,3072]{1,0:T(8,128)(2,1)} %bitcast.16, bf16[384,512]{1,0:T(8,128)(2,1)} %get-tuple-element.31.turned_ref, f32[8,384]{1,0:T(8,128)} %get-tuple-element.32.sums_ref, ...), custom_call_target="tpu_custom_call" | custom-call | tf_op jit(solution)/shard_map/cotangents/pallas_call | solution.py:771
  245.9 8.0 %attend_back.3.grad_ref = bf16[3,512,384]{2,1,0:T(8,128)(2,1)} custom-call(f32[512,1152]{1,0:T(8,128)} %get-tuple-element.22.q_ref.k_ref.v_ref, f32[512,1152]{1,0:T(8,128)} %get-tuple-element.22.q_ref.k_ref.v_ref, f32[512,1152]{1,0:T(8,128)} %get-tuple-element.22.q_ref.k_ref.v_ref, f32[2,128]{1,0:T(2,128)} %bitcast.27, f32[512,384]{1,0:T(8,128)} %get-tuple-element.34.grad_ref), custom_call_target="tpu_custom_call" | custom-call | tf_op jit(solution)/shard_map/attend_back/pallas_call | solution.py:419
  254.0 0.0 copy-start.1
  254.0 0.0 copy-start
  254.0 14.4 %weight_grads.1 = bf16[3,3072,384]{2,1,0:T(8,128)(2,1)} custom-call(bf16[3072,512]{1,0:T(8,128)(2,1)} %get-tuple-element.25.turned_ref, bf16[3,512,384]{2,1,0:T(8,128)(2,1)} %attend_back.3.grad_ref, bf16[3,3072,384]{2,1,0:T(8,128)(2,1)} %get-tuple-element.35.part_ref), custom_call_target="tpu_custom_call" | custom-call | tf_op jit(solution)/shard_map/weight_grads/pallas_call | solution.py:793
  268.4 0.0 copy-done.1
  268.4 0.7 copy.16
  269.1 0.0 copy-done
  269.1 0.0 copy-start.2
  269.1 1.4 copy.17
  270.5 0.0 copy-done.2
  270.5 0.7 copy.18
Async XLA Ops:
  254.0 14.4 %copy-start.1 = (bf16[64,3072]{1,0:T(8,128)(2,1)S(1)}, bf16[64,3072]{1,0:T(8,128)(2,1)}, u32[]{:S(2)}) copy-start(bf16[64,3072]{1,0:T(8,128)(2,1)} %get-tuple-element.24) | copy-start | bytes 1179652
  254.0 15.2 %copy-start = (bf16[384,3072]{1,0:T(8,128)(2,1)S(1)}, bf16[384,3072]{1,0:T(8,128)(2,1)}, u32[]{:S(2)}) copy-start(bf16[384,3072]{1,0:T(8,128)(2,1)} %get-tuple-element.36) | copy-start | bytes 7077892
  269.1 1.4 copy-start.2
where the time goes:
time: 273 us; the launch traced here: 271 us
  Pallas kernels  265 us (97%)
  local copies, waits for them, and re-layouts  5.55 us (2%)
    pallas_call x2, Pallas kernels, project(): pl.pallas_call(project_kernel, out_shape=(jax.ShapeDtypeStruct((TOTAL, 3...  69.5 us
    pallas_call x1, Pallas kernels, input_grads(): pl.pallas_call(input_grad_kernel, out_shape=jax.ShapeDtypeStruct((ROWS, D...  50.9 us
    pallas_call x1, Pallas kernels, cotangents(): pl.pallas_call(cotangent_kernel, out_shape=(jax.ShapeDtypeStruct((TOTAL,...  43 us
    pallas_call x1, Pallas kernels, out_rows(): pl.pallas_call(out_kernel, out_shape=(jax.ShapeDtypeStruct((ROWS, D), bf1...  42.7 us
    pallas_call x2, Pallas kernels, attend_back(): pl.pallas_call(functools.partial(attend_back_kernel, shared), grid=(2, 3)...  15.9 us
    pallas_call x1, Pallas kernels, classify(): pl.pallas_call(head_kernel, out_shape=(jax.ShapeDtypeStruct((8, 128), f32...  15 us
    pallas_call x1, Pallas kernels, weight_grads(): pl.pallas_call(weight_kernel, grid=(D // tall, 3), out_shape=jax.ShapeDty...  14.4 us
    pallas_call x2, Pallas kernels, attend(): pl.pallas_call(attend_kernel, grid=(2, 3), out_shape=(jax.ShapeDtypeStruc...  13.5 us

commit v1 on v0

v1 whole, which is shorter than its diff:
```python
import functools
import math

import jax
import jax.numpy as jnp
from jax import lax
from jax.experimental import pallas as pl
from jax.experimental.pallas import tpu as pltpu
from jax.sharding import PartitionSpec as P

HS = 128
PATCHES = 256
EPS = 1e-06
N_DP = 4
N_T = 2
ROWS = 64
TOTAL = 512
D = 3072
F = 384
CLASSES = 512
W = 512
CHUNKS = D // W
AHEAD = 2
KINDS = ("A", "B", "A", "A", "B", "A")
MESH = pl.DeviceIdType.MESH
f32 = jnp.float32
bf16 = jnp.bfloat16
VM = pl.BlockSpec(memory_space=pltpu.VMEM)
ANY = pl.BlockSpec(memory_space=pl.ANY)


def dot_nn(a, b):
    return lax.dot_general(a, b, (((1,), (0,)), ((), ())), preferred_element_type=f32)


def dot_nt(a, b):
    return lax.dot_general(a, b, (((1,), (1,)), ((), ())), preferred_element_type=f32)


def norm_last(values, gain_row):
    centered = values - jnp.mean(values, axis=-1, keepdims=True)
    inverse = lax.rsqrt(jnp.mean(centered * centered, axis=-1, keepdims=True) + EPS)
    unit_rows = centered * inverse
    return unit_rows * gain_row, unit_rows, inverse


def norm_back(grad, unit_rows, inverse, gain_row):
    scaled = grad * gain_row
    return inverse * (
        scaled
        - jnp.mean(scaled, axis=-1, keepdims=True)
        - unit_rows * jnp.mean(scaled * unit_rows, axis=-1, keepdims=True)
    )


def place():
    return lax.axis_index("dp"), lax.axis_index("tensor")


def neighbour(dz, dt):
    z, t = place()
    target = {}
    if dz:
        target["dp"] = lax.rem(z + dz + N_DP, N_DP)
    if dt:
        target["tensor"] = 1 - t
    return target


def section_at(step):
    s, n = lax.axis_index("section"), lax.axis_size("section")
    return {"section": lax.rem(s + step + n, n)}


def enter(devices):
    barrier = pltpu.get_barrier_semaphore()
    for device in devices:
        pl.semaphore_signal(barrier, inc=1, device_id=device, device_id_type=MESH)
    pl.semaphore_wait(barrier, len(devices))


def rows_of(dz, dt):
    z, t = place()
    owner = lax.rem(z + dz + N_DP, N_DP) * N_T + ((1 - t) if dt else t)
    return pl.ds(pl.multiple_of(owner * ROWS, ROWS), ROWS)


def columns(c):
    return pl.ds(c * W, W)


class Gather:
    def __init__(self, buf, send_sem, recv_sem):
        self.buf, self.send_sem, self.recv_sem = buf, send_sem, recv_sem
        self.sent = []

    def view(self, dz, dt, c):
        return self.buf.at[rows_of(dz, dt), columns(c)]

    def send(self, c, dz, dt, to_z, to_t):
        k = sum(1 for (cc, _) in self.sent if cc == c)
        slot = ((dz - to_z) % N_DP) * 2 + (dt ^ to_t)
        part = self.view(dz, dt, c)
        copy = pltpu.make_async_remote_copy(
            src_ref=part,
            dst_ref=part,
            send_sem=self.send_sem.at[c, k],
            recv_sem=self.recv_sem.at[c, slot],
            device_id=neighbour(to_z, to_t),
            device_id_type=MESH,
        )
        copy.start()
        self.sent.append((c, copy))

    def recv(self, c, dz, dt):
        part = self.view(dz, dt, c)
        pltpu.make_async_remote_copy(
            src_ref=part,
            dst_ref=part,
            send_sem=self.send_sem.at[c, 0],
            recv_sem=self.recv_sem.at[c, (dz % N_DP) * 2 + dt],
            device_id=neighbour(1, 0),
            device_id_type=MESH,
        ).wait_recv()

    def begin(self, c):
        if KINDS[c] == "A":
            self.send(c, 0, 0, 0, 1)
            self.send(c, 0, 0, 1, 0)
            self.send(c, 0, 0, -1, 0)
        else:
            self.send(c, 0, 0, 1, 0)
            self.send(c, 0, 0, -1, 0)
            self.send(c, 0, 0, 0, 1)

    def first(self, c):
        if KINDS[c] == "A":
            self.recv(c, 0, 1)
            self.send(c, 0, 1, 1, 0)
            self.send(c, 0, 1, -1, 0)
            self.recv(c, -1, 0)
            self.send(c, -1, 0, 1, 0)
        else:
            way = 1 if c % 2 else -1
            self.recv(c, -way, 0)
            self.send(c, -way, 0, way, 0)
            self.send(c, -way, 0, 0, 1)
            self.recv(c, way, 0)
            self.send(c, way, 0, 0, 1)

    def second(self, c):
        if KINDS[c] == "A":
            self.recv(c, 1, 1)
            self.send(c, 1, 1, -1, 0)
        else:
            self.recv(c, 2, 0)
            self.send(c, 2, 0, 0, 1)

    def third(self, c):
        if KINDS[c] == "A":
            rest = ((1, 0), (-1, 1), (2, 0), (2, 1))
        else:
            rest = ((0, 1), (-1, 1), (1, 1), (2, 1))
        for dz, dt in rest:
            self.recv(c, dz, dt)

    def run(self, compute, side=None):
        for c in range(AHEAD):
            self.begin(c)
        for i in range(CHUNKS + 2):
            if i < CHUNKS:
                self.first(i)
            if i + AHEAD < CHUNKS:
                self.begin(i + AHEAD)
            if side is not None:
                side(i)
            if 0 <= i - 1 < CHUNKS:
                self.second(i - 1)
            if i >= 2:
                self.third(i - 2)
                compute(i - 2)

    def finish(self):
        for _, copy in self.sent:
            copy.wait_send()


RING = ((1, 0), (-1, 0), (0, 1))


class Scatter:
    def __init__(self, part, land, send_sem, recv_sem):
        self.part, self.land = part, land
        self.send_sem, self.recv_sem = send_sem, recv_sem
        self.sent = []

    def view(self, dz, dt, c):
        return self.part.at[rows_of(dz, dt), columns(c)]

    def send(self, c, dz, dt, to_z, to_t, slot):
        copy = pltpu.make_async_remote_copy(
            src_ref=self.view(dz, dt, c),
            dst_ref=self.land.at[c, slot],
            send_sem=self.send_sem.at[c, slot],
            recv_sem=self.recv_sem.at[c, slot],
            device_id=neighbour(to_z, to_t),
            device_id_type=MESH,
        )
        copy.start()
        self.sent.append(copy)

    def recv(self, c, slot):
        pltpu.make_async_remote_copy(
            src_ref=self.view(0, 0, c),
            dst_ref=self.land.at[c, slot],
            send_sem=self.send_sem.at[c, slot],
            recv_sem=self.recv_sem.at[c, slot],
            device_id=neighbour(1, 0),
            device_id_type=MESH,
        ).wait_recv()
        return self.land[c, slot].astype(f32)

    def value(self, dz, dt, c):
        return self.part[rows_of(dz, dt), columns(c)].astype(f32)

    def put(self, dz, dt, c, value):
        self.part[rows_of(dz, dt), columns(c)] = value.astype(bf16)

    def begin(self, c):
        if KINDS[c] == "A":
            self.send(c, 2, 0, 1, 0, 0)
            self.send(c, 2, 1, -1, 0, 1)
            self.send(c, -1, 0, -1, 0, 2)
            self.send(c, 1, 1, 1, 0, 3)
        else:
            self.send(c, 2, 1, 0, 1, 0)
            self.send(c, 1, 1, 0, 1, 1)
            self.send(c, -1, 1, 0, 1, 2)
            self.send(c, 0, 1, 0, 1, 3)

    def first(self, c):
        if KINDS[c] == "A":
            self.put(1, 0, c, self.value(1, 0, c) + self.recv(c, 0))
            self.send(c, 1, 0, 1, 0, 4)
            self.put(-1, 1, c, self.value(-1, 1, c) + self.recv(c, 1))
            self.send(c, -1, 1, -1, 0, 5)
        else:
            way = 1 if c % 2 else -1
            self.put(2, 0, c, self.value(2, 0, c) + self.recv(c, 0))
            self.send(c, 2, 0, way, 0, 4)
            other = 2 if way == 1 else 1
            self.put(-way, 0, c, self.value(-way, 0, c) + self.recv(c, other))
            self.send(c, -way, 0, -way, 0, 5)

    def second(self, c):
        if KINDS[c] == "A":
            total = self.value(0, 1, c) + self.recv(c, 3) + self.recv(c, 5)
            self.put(0, 1, c, total)
            self.send(c, 0, 1, 0, 1, 6)
        else:
            way = 1 if c % 2 else -1
            other = 1 if way == 1 else 2
            total = self.value(way, 0, c) + self.recv(c, other) + self.recv(c, 4)
            self.put(way, 0, c, total)
            self.send(c, way, 0, way, 0, 6)

    def third(self, c):
        rest = (2, 4, 6) if KINDS[c] == "A" else (3, 5, 6)
        total = self.value(0, 0, c)
        for slot in rest:
            total = total + self.recv(c, slot)
        return total

    def run(self, compute, done):
        for i in range(CHUNKS + 3):
            if i < CHUNKS:
                compute(i)
                self.begin(i)
            if 0 <= i - 1 < CHUNKS:
                self.first(i - 1)
            if 0 <= i - 2 < CHUNKS:
                self.second(i - 2)
            if 0 <= i - 3:
                done(i - 3, self.third(i - 3))

    def finish(self):
        for copy in self.sent:
            copy.wait_send()


def params(collective_id=None, limit=62 * 1024 * 1024):
    if collective_id is None:
        return pltpu.CompilerParams(vmem_limit_bytes=limit)
    return pltpu.CompilerParams(
        collective_id=collective_id, has_side_effects=True, vmem_limit_bytes=limit
    )


def ring_sems():
    return [pltpu.SemaphoreType.DMA((CHUNKS, 8)), pltpu.SemaphoreType.DMA((CHUNKS, 8))]


def land_scratch():
    return [pltpu.VMEM((TOTAL, D), bf16), pltpu.VMEM((CHUNKS, 7, ROWS, W), bf16)]


def image_rows(i):
    return pl.ds(pl.multiple_of(i * PATCHES, PATCHES), PATCHES)


def project_chunk(buf, wbuf, proj, turned, c):
    def tile(r, carry):
        rows = image_rows(r)
        block = buf[rows, columns(c)]
        for t in range(3):
            value = dot_nn(block, wbuf[t, columns(c), :])
            cols = pl.ds(t * F, F)
            if c == 0:
                proj[rows, cols] = value
            else:
                proj[rows, cols] += value
        turned[columns(c), rows] = block.T
        return carry

    lax.fori_loop(0, TOTAL // PATCHES, tile, 0)


def head_cols(t, h):
    return pl.ds(t * F + h * HS, HS)


def head_state(q, k, v, pair):
    q_normed, q_unit, q_inv = norm_last(q, pair[0:1, :])
    k_normed, k_unit, k_inv = norm_last(k, pair[1:2, :])
    q_half, k_half = q_normed.astype(bf16), k_normed.astype(bf16)
    v_half = v.astype(bf16)
    exponent = jnp.exp(dot_nt(q_half, k_half) * (1.0 / math.sqrt(HS)))
    probs = exponent * (1.0 / jnp.sum(exponent, axis=-1, keepdims=True))
    return q_unit, q_inv, k_unit, k_inv, q_half, k_half, v_half, probs


def state_of(proj, pair, rows, h):
    return head_state(*[proj[rows, head_cols(t, h)] for t in range(3)], pair)


def attend(proj, pair_ref, att, turned):
    def image(i, carry):
        rows = image_rows(i)
        for h in range(3):
            v_half, probs = state_of(proj, pair_ref[...], rows, h)[-2:]
            mixed = dot_nn(probs.astype(bf16), v_half)
            att[rows, pl.ds(h * HS, HS)] = mixed.astype(bf16)
            if turned is not None:
                turned[pl.ds(h * HS, HS), rows] = mixed.T.astype(bf16)
        return carry

    lax.fori_loop(0, 2, image, 0)


def back_of_head(state, pair, mixed):
    q_unit, q_inv, k_unit, k_inv, q_half, k_half, v_half, probs = state
    grad_probs = dot_nt(mixed, v_half)
    grad_value = dot_nn(probs.T.astype(bf16), mixed)
    grad_scores = probs * (grad_probs - jnp.sum(probs * grad_probs, axis=-1, keepdims=True))
    scaled = grad_scores * (1.0 / math.sqrt(HS))
    grad_query = dot_nn(scaled.astype(bf16), k_half)
    grad_key = dot_nn(scaled.T.astype(bf16), q_half)
    return (
        norm_back(grad_query, q_unit, q_inv, pair[0:1, :]).astype(bf16),
        norm_back(grad_key, k_unit, k_inv, pair[1:2, :]).astype(bf16),
        grad_value.astype(bf16),
    )


PEERS = tuple((dz, dt) for dz in range(N_DP) for dt in range(N_T) if dz or dt)
PACK = D // 4


def front_kernel(
    rows_ref,
    gain_ref,
    pair_ref,
    pool_ref,
    label_ref,
    w_hbm,
    wout_hbm,
    head_hbm,
    out_ref,
    margin_ref,
    proj_hbm,
    turned_hbm,
    att_turned_ref,
    margin_turned_hbm,
    margin_grad_ref,
    head_grad_ref,
    image_ref,
    sums_ref,
    loss_ref,
    wbuf,
    wout,
    head,
    buf_own,
    buf_margin,
    proj_own,
    proj_margin,
    turned_own,
    turned_margin,
    att,
    part,
    land,
    next_rows,
    stage,
    pool_land,
    pooled_ref,
    half_ref,
    per_image,
    load_sem,
    store_sem,
    own_send,
    own_recv,
    sum_send,
    sum_recv,
    step_send,
    step_recv,
    margin_send,
    margin_recv,
    pool_send,
    pool_recv,
):
    load_w = pltpu.make_async_copy(w_hbm, wbuf, load_sem.at[0])
    load_out = pltpu.make_async_copy(wout_hbm, wout, load_sem.at[1])
    load_head = pltpu.make_async_copy(head_hbm, head, load_sem.at[2])
    load_w.start()
    load_out.start()
    load_head.start()
    normed, _, _ = norm_last(rows_ref[...].astype(f32), gain_ref[...])
    buf_own[rows_of(0, 0), :] = normed.astype(bf16)
    enter([neighbour(*way) for way in PEERS] + [section_at(1), section_at(-1)])

    gather = Gather(buf_own, own_send, own_recv)

    def compute_own(c):
        if c == 0:
            load_w.wait()
        project_chunk(buf_own, wbuf, proj_own, turned_own, c)

    gather.run(compute_own)
    stores = [
        pltpu.make_async_copy(proj_own, proj_hbm, store_sem.at[0]),
        pltpu.make_async_copy(turned_own, turned_hbm, store_sem.at[1]),
    ]
    for store in stores:
        store.start()
    attend(proj_own, pair_ref, att, att_turned_ref)

    load_out.wait()
    scatter = Scatter(part, land, sum_send, sum_recv)
    hops = []

    def out_chunk(c):
        def tile(r, carry):
            rows = image_rows(r)
            part[rows, columns(c)] = dot_nn(att[rows, :], wout[:, columns(c)]).astype(bf16)
            return carry

        lax.fori_loop(0, TOTAL // PATCHES, tile, 0)

    def out_done(c, total):
        out_ref[:, columns(c)] = (rows_ref[:, columns(c)].astype(f32) + total).astype(bf16)
        copy = pltpu.make_async_remote_copy(
            src_ref=out_ref.at[:, columns(c)],
            dst_ref=next_rows.at[:, columns(c)],
            send_sem=step_send.at[c],
            recv_sem=step_recv.at[c],
            device_id=section_at(1),
            device_id_type=MESH,
        )
        copy.start()
        hops.append(copy)

    scatter.run(out_chunk, out_done)
    for copy in hops:
        copy.wait_recv()
    first = lax.axis_index("section") == 0
    margin = jnp.where(first, rows_ref[...], next_rows[...])
    margin_ref[...] = margin
    normed, _, _ = norm_last(margin.astype(f32), gain_ref[...])
    buf_margin[rows_of(0, 0), :] = normed.astype(bf16)
    second = Gather(buf_margin, margin_send, margin_recv)
    second.run(lambda c: project_chunk(buf_margin, wbuf, proj_margin, turned_margin, c))
    store = pltpu.make_async_copy(turned_margin, margin_turned_hbm, store_sem.at[2])
    store.start()
    stores.append(store)
    attend(proj_margin, pair_ref, att, None)

    row_id = lax.broadcasted_iota(jnp.int32, (8, 1), 0)
    sums_ref[...] = jnp.zeros_like(sums_ref)
    for i in range(2):
        block = att[i * PATCHES : (i + 1) * PATCHES, :].astype(f32)
        sums_ref[i : i + 1, :] = jnp.sum(block, axis=0, keepdims=True)
    sums = sums_ref[...]
    hi = sums.astype(bf16).astype(f32)
    mid = (sums - hi).astype(bf16).astype(f32)
    low = sums - hi - mid
    tall = jnp.concatenate([hi, mid, low], axis=0).astype(bf16)
    terms = dot_nn(tall, wout[...])
    partial_rows = terms[0:8] + terms[8:16] + terms[16:24]
    own = jnp.sum(margin_ref[...].astype(f32), axis=0, keepdims=True)
    image = lax.axis_index("dp") // (N_DP // 2)
    partial_rows = partial_rows + jnp.where(row_id == image, own, 0.0)
    for i in range(2):
        for q in range(4):
            stage[i * 4 + q : i * 4 + q + 1, :] = partial_rows[i : i + 1, q * PACK : (q + 1) * PACK]
    copies = []
    for k, way in enumerate(PEERS):
        copy = pltpu.make_async_remote_copy(
            src_ref=stage,
            dst_ref=pool_land.at[k],
            send_sem=pool_send.at[k],
            recv_sem=pool_recv.at[k],
            device_id=neighbour(*way),
            device_id_type=MESH,
        )
        copy.start()
        copies.append(copy)
    load_head.wait()
    total = stage[...]
    for k, copy in enumerate(copies):
        copy.wait_recv()
        total = total + pool_land[k]
    pooled_ref[...] = jnp.zeros_like(pooled_ref)
    for i in range(2):
        for q in range(4):
            pooled_ref[i : i + 1, q * PACK : (q + 1) * PACK] = total[i * 4 + q : i * 4 + q + 1, :]
    gain = pool_ref[...]
    normed, unit_rows, inverse = norm_last(pooled_ref[...] / PATCHES, gain)
    half = normed.astype(bf16)
    half_ref[...] = half.astype(f32)
    logits = dot_nn(half, head[...])
    label = jnp.where(row_id == 0, label_ref[0:1, 0:1], label_ref[0:1, 1:2])
    targets = (label == lax.broadcasted_iota(jnp.int32, (8, CLASSES), 1)).astype(f32)
    soft = jnp.maximum(logits, 0.0) + jnp.log1p(jnp.exp(-jnp.abs(logits)))
    loss = jnp.mean(soft - targets * logits, axis=-1, keepdims=True)
    lane = lax.broadcasted_iota(jnp.int32, (8, 128), 1)
    loss_ref[...] = jnp.sum(jnp.where(row_id == lane, loss, 0.0), axis=0, keepdims=True)[:, 0:2]
    grad_logits = (jax.nn.sigmoid(logits) - targets) / 2
    grad_logits = jnp.where(row_id < 2, grad_logits, 0.0).astype(bf16)
    grad_pooled = norm_back(dot_nt(grad_logits, head[...]), unit_rows, inverse, gain)
    grad_image = grad_pooled / PATCHES
    image_ref[...] = jnp.where(row_id < 2, grad_image, 0.0)
    per_image[...] = dot_nt(grad_image.astype(bf16), wout[...])
    z, t = place()
    width = D // (N_DP * N_T)
    start = pl.multiple_of((z * N_T + t) * width, width)
    mine = half_ref[:, pl.ds(start, width)]
    head_grad_ref[...] = dot_nn(mine.T.astype(bf16), grad_logits).astype(bf16)

    def back_image(i, carry):
        rows = image_rows(i)
        for h in range(3):
            state = state_of(proj_margin, pair_ref[...], rows, h)
            row = jnp.where(i == 0, per_image[0:1, pl.ds(h * HS, HS)], per_image[1:2, pl.ds(h * HS, HS)])
            mixed = jnp.broadcast_to(row, (PATCHES, HS)).astype(bf16)
            for t, value in enumerate(back_of_head(state, pair_ref[...], mixed)):
                margin_grad_ref[t, rows, pl.ds(h * HS, HS)] = value
        return carry

    lax.fori_loop(0, 2, back_image, 0)
    gather.finish()
    scatter.finish()
    second.finish()
    for copy in hops + copies:
        copy.wait_send()
    for store in stores:
        store.wait()


def front(rows, gain_row, gain_pair, pool_row, labels, qkv_local, out_local, head_local, collective_id):
    return pl.pallas_call(
        front_kernel,
        out_shape=(
            jax.ShapeDtypeStruct((ROWS, D), bf16),
            jax.ShapeDtypeStruct((ROWS, D), bf16),
            jax.ShapeDtypeStruct((TOTAL, 3 * F), f32),
            jax.ShapeDtypeStruct((D, TOTAL), bf16),
            jax.ShapeDtypeStruct((F, TOTAL), bf16),
            jax.ShapeDtypeStruct((D, TOTAL), bf16),
            jax.ShapeDtypeStruct((3, TOTAL, F), bf16),
            jax.ShapeDtypeStruct((F, CLASSES), bf16),
            jax.ShapeDtypeStruct((8, D), f32),
            jax.ShapeDtypeStruct((8, F), f32),
            jax.ShapeDtypeStruct((1, 2), f32),
        ),
        in_specs=[VM, VM, VM, VM, VM, ANY, ANY, ANY],
        out_specs=(VM, VM, ANY, ANY, VM, ANY, VM, VM, VM, VM, VM),
        scratch_shapes=[
            pltpu.VMEM((3, D, F), bf16),
            pltpu.VMEM((F, D), bf16),
            pltpu.VMEM((D, CLASSES), bf16),
            pltpu.VMEM((TOTAL, D), bf16),
            pltpu.VMEM((TOTAL, D), bf16),
            pltpu.VMEM((TOTAL, 3 * F), f32),
            pltpu.VMEM((TOTAL, 3 * F), f32),
            pltpu.VMEM((D, TOTAL), bf16),
            pltpu.VMEM((D, TOTAL), bf16),
            pltpu.VMEM((TOTAL, F), bf16),
        ]
        + land_scratch()
        + [
            pltpu.VMEM((ROWS, D), bf16),
            pltpu.VMEM((8, PACK), f32),
            pltpu.VMEM((len(PEERS), 8, PACK), f32),
            pltpu.VMEM((8, D), f32),
            pltpu.VMEM((8, D), f32),
            pltpu.VMEM((8, F), f32),
            pltpu.SemaphoreType.DMA((3,)),
            pltpu.SemaphoreType.DMA((3,)),
        ]
        + ring_sems()
        + ring_sems()
        + [pltpu.SemaphoreType.DMA((CHUNKS,)), pltpu.SemaphoreType.DMA((CHUNKS,))]
        + ring_sems()
        + [pltpu.SemaphoreType.DMA((len(PEERS),)), pltpu.SemaphoreType.DMA((len(PEERS),))],
        compiler_params=params(collective_id),
        name="front",
    )(rows, gain_row, gain_pair, pool_row, labels, qkv_local, out_local, head_local)


def back_kernel(
    grad_ref,
    rows_ref,
    gain_ref,
    image_ref,
    sums_ref,
    w_hbm,
    wout_hbm,
    turned_hbm,
    margin_turned_hbm,
    grad_att_ref,
    grad_out_hbm,
    margin_part_hbm,
    part,
    land,
    wbuf,
    wout,
    turned,
    margin_turned,
    total_ref,
    mine,
    came,
    buf,
    grad_out,
    margin_part,
    wsem,
    load_sem,
    out_sem,
    part_sem,
    sum_send,
    sum_recv,
    step_send,
    step_recv,
    own_send,
    own_recv,
):
    loads = []
    for c in range(CHUNKS):
        load = pltpu.make_async_copy(
            w_hbm.at[:, columns(c), :], wbuf.at[:, columns(c), :], wsem.at[c]
        )
        load.start()
        loads.append(load)
    later = [
        pltpu.make_async_copy(margin_turned_hbm, margin_turned, load_sem.at[0]),
        pltpu.make_async_copy(wout_hbm, wout, load_sem.at[1]),
        pltpu.make_async_copy(turned_hbm, turned, load_sem.at[2]),
    ]
    for load in later:
        load.start()
    enter([neighbour(*way) for way in RING] + [section_at(1), section_at(-1)])
    scatter = Scatter(part, land, sum_send, sum_recv)

    def compute(c):
        loads[c].wait()

        def tile(r, carry):
            rows = image_rows(r)
            value = dot_nt(grad_ref[0, rows, :], wbuf[0, columns(c), :])
            value = value + dot_nt(grad_ref[1, rows, :], wbuf[1, columns(c), :])
            value = value + dot_nt(grad_ref[2, rows, :], wbuf[2, columns(c), :])
            part[rows, columns(c)] = value.astype(bf16)
            return carry

        lax.fori_loop(0, TOTAL // PATCHES, tile, 0)

    def done(c, total):
        total_ref[:, columns(c)] = total

    scatter.run(compute, done)
    gain = gain_ref[...]
    _, unit_rows, inverse = norm_last(rows_ref[...].astype(f32), gain)
    image = lax.axis_index("dp") // (N_DP // 2)
    residual = jnp.where(image == 0, image_ref[0:1, :], image_ref[1:2, :])
    grad = residual + norm_back(total_ref[...], unit_rows, inverse, gain)
    mine[...] = grad.astype(bf16)
    copies = []
    for c in range(CHUNKS):
        copy = pltpu.make_async_remote_copy(
            src_ref=mine.at[:, columns(c)],
            dst_ref=came.at[:, columns(c)],
            send_sem=step_send.at[c],
            recv_sem=step_recv.at[c],
            device_id=section_at(-1),
            device_id_type=MESH,
        )
        copy.start()
        copies.append(copy)
    for load in later:
        load.wait()
    last = lax.axis_index("section") == lax.axis_size("section") - 1

    gather = Gather(buf, own_send, own_recv)
    begin = gather.begin

    def begin_after_hop(c):
        copies[c].wait_recv()
        block = came[:, columns(c)]
        buf[rows_of(0, 0), columns(c)] = jnp.where(last, jnp.zeros_like(block), block)
        begin(c)

    gather.begin = begin_after_hop
    sums_t = sums_ref[...].T
    hi = sums_t.astype(bf16)
    low = (sums_t - hi.astype(f32)).astype(bf16)
    stores = []

    def margin_piece(c):
        if c >= CHUNKS:
            return

        def margin_tile(r, carry):
            rows = pl.ds(pl.multiple_of(c * W + r * 256, 256), 256)
            for t in range(3):
                margin_part[t, rows, :] = dot_nn(margin_turned[rows, :], grad_ref[t]).astype(bf16)
            return carry

        lax.fori_loop(0, W // 256, margin_tile, 0)
        store = pltpu.make_async_copy(
            margin_part.at[:, columns(c), :], margin_part_hbm.at[:, columns(c), :], part_sem.at[c]
        )
        store.start()
        stores.append(store)

    def chunk(c):
        def tile(r, carry):
            rows = image_rows(r)
            value = dot_nt(buf[rows, columns(c)], wout[:, columns(c)])
            if c == 0:
                grad_att_ref[rows, :] = value
            else:
                grad_att_ref[rows, :] += value
            return carry

        lax.fori_loop(0, TOTAL // PATCHES, tile, 0)
        shared = image_ref[:, columns(c)].astype(bf16)
        value = dot_nn(turned[...], buf[:, columns(c)])
        value = value + dot_nn(hi, shared) + dot_nn(low, shared)
        grad_out[:, columns(c)] = value.astype(bf16)
        store = pltpu.make_async_copy(
            grad_out.at[:, columns(c)], grad_out_hbm.at[:, columns(c)], out_sem.at[c]
        )
        store.start()
        stores.append(store)

    gather.run(chunk, margin_piece)
    scatter.finish()
    gather.finish()
    for copy in copies:
        copy.wait_send()
    for store in stores:
        store.wait()


def back(grad, rows, gain_row, grad_image, sums, qkv_local, out_local, turned, margin_turned, collective_id):
    return pl.pallas_call(
        back_kernel,
        out_shape=(
            jax.ShapeDtypeStruct((TOTAL, F), f32),
            jax.ShapeDtypeStruct((F, D), bf16),
            jax.ShapeDtypeStruct((3, D, F), bf16),
        ),
        in_specs=[VM] * 5 + [ANY] * 4,
        out_specs=(VM, ANY, ANY),
        scratch_shapes=land_scratch()
        + [
            pltpu.VMEM((3, D, F), bf16),
            pltpu.VMEM((F, D), bf16),
            pltpu.VMEM((F, TOTAL), bf16),
            pltpu.VMEM((D, TOTAL), bf16),
            pltpu.VMEM((ROWS, D), f32),
            pltpu.VMEM((ROWS, D), bf16),
            pltpu.VMEM((ROWS, D), bf16),
            pltpu.VMEM((TOTAL, D), bf16),
            pltpu.VMEM((F, D), bf16),
            pltpu.VMEM((3, D, F), bf16),
            pltpu.SemaphoreType.DMA((CHUNKS,)),
            pltpu.SemaphoreType.DMA((3,)),
            pltpu.SemaphoreType.DMA((CHUNKS,)),
            pltpu.SemaphoreType.DMA((CHUNKS,)),
        ]
        + ring_sems()
        + [pltpu.SemaphoreType.DMA((CHUNKS,)), pltpu.SemaphoreType.DMA((CHUNKS,))]
        + ring_sems(),
        compiler_params=params(collective_id),
        name="back",
    )(grad, rows, gain_row, grad_image, sums, qkv_local, out_local, turned, margin_turned)


def own_back_kernel(proj_ref, pair_ref, grad_ref, out_ref):
    rows = pl.ds(0, PATCHES)
    for h in range(3):
        cols = pl.ds(h * HS, HS)
        state = state_of(proj_ref, pair_ref[...], rows, h)
        mixed = grad_ref[:, cols].astype(bf16)
        for t, value in enumerate(back_of_head(state, pair_ref[...], mixed)):
            out_ref[t, :, cols] = value


def own_back(projected, gain_pair, grad):
    return pl.pallas_call(
        own_back_kernel,
        grid=(2,),
        out_shape=jax.ShapeDtypeStruct((3, TOTAL, F), bf16),
        in_specs=[
            pl.BlockSpec((PATCHES, 3 * F), lambda i: (i, 0)),
            pl.BlockSpec((2, HS), lambda i: (0, 0)),
            pl.BlockSpec((PATCHES, F), lambda i: (i, 0)),
        ],
        out_specs=pl.BlockSpec((3, PATCHES, F), lambda i: (0, i, 0)),
        compiler_params=params(),
        name="own_back",
    )(projected, gain_pair, grad)


def weight_kernel(turned_ref, grad_ref, part_ref, *refs):
    count = len(refs) // 2
    passed, out_ref = refs[:count], refs[count]
    for t in range(3):
        value = dot_nn(turned_ref[...], grad_ref[t]) + part_ref[t].astype(f32)
        out_ref[t] = value.astype(bf16)
    for source, target in zip(passed, refs[count + 1 :]):
        target[...] = source[...]


def weight_grads(turned, projection_gradient, margin_part, passed):
    steps = 12
    tall = D // steps
    specs = [
        pl.BlockSpec((ROWS, D // steps), lambda r: (0, r)),
        pl.BlockSpec((F, D // steps), lambda r: (0, r)),
        pl.BlockSpec((F // steps, CLASSES), lambda r: (r, 0)),
    ]
    return pl.pallas_call(
        weight_kernel,
        grid=(steps,),
        out_shape=[jax.ShapeDtypeStruct((3, D, F), bf16)]
        + [jax.ShapeDtypeStruct(x.shape, x.dtype) for x in passed],
        in_specs=[
            pl.BlockSpec((tall, TOTAL), lambda r: (r, 0)),
            pl.BlockSpec((3, TOTAL, F), lambda r: (0, 0, 0)),
            pl.BlockSpec((3, tall, F), lambda r: (0, r, 0)),
        ]
        + specs,
        out_specs=[pl.BlockSpec((3, tall, F), lambda r: (0, r, 0))] + specs,
        compiler_params=params(),
        name="weight_grads",
    )(turned, projection_gradient, margin_part, *passed)


def on_device(
    block_inputs, qkv_weights, out_weights, norm_gain, query_key_gain, pool_gain, class_head, labels
):
    rows_in, qkv_local, out_local = block_inputs[0], qkv_weights[0], out_weights[0]
    gain_pair = query_key_gain[0]
    (
        out_own,
        margin_rows,
        projected,
        turned,
        attention_turned,
        margin_turned,
        margin_grad,
        grad_head,
        grad_image,
        sums,
        losses,
    ) = front(
        rows_in, norm_gain, gain_pair, pool_gain, labels, qkv_local, out_local, class_head[0], 0
    )
    grad_attention, grad_out, margin_part = back(
        margin_grad,
        margin_rows,
        norm_gain,
        grad_image,
        sums,
        qkv_local,
        out_local,
        attention_turned,
        margin_turned,
        1,
    )
    own_grad = own_back(projected, gain_pair, grad_attention)
    qkv_grad, out_own, grad_out, grad_head = weight_grads(
        turned, own_grad, margin_part, (out_own, grad_out, grad_head)
    )
    return (out_own[None], qkv_grad[None], grad_out[None], grad_head[None], losses)


def solution(mesh):
    in_specs = (
        P("section", ("dp", "tensor"), None),
        P("section", None, None, ("dp", "tensor")),
        P("section", ("dp", "tensor"), None),
        P("section", None),
        P("section", None, None),
        P("section", None),
        P("section", None, None),
        P("section", None),
    )
    out_specs = (
        P("section", ("dp", "tensor"), None),
        P("section", None, None, ("dp", "tensor")),
        P("section", ("dp", "tensor"), None),
        P("section", ("dp", "tensor"), None),
        P("section", None),
    )
    return jax.shard_map(
        on_device, mesh=mesh, in_specs=in_specs, out_specs=out_specs, check_vma=False
    )
```

time: 273 us -> 218 us (0.80)
  Pallas kernels: 265 us -> 215 us
  local copies, waits for them, and re-layouts: 5.55 us -> 0.52 us
    pallas_call x11 -> x4, Pallas kernels: 265 us -> 215 us  [the longest x1 120 us: front(): pl.pallas_call(front_kernel, out_shape=(jax.ShapeDtypeStruct((ROWS, D), b...]
where the time goes in v1:
time: 218 us; the launch traced here: 217 us
  Pallas kernels  215 us (99%)
    pallas_call x1, Pallas kernels, front(): pl.pallas_call(front_kernel, out_shape=(jax.ShapeDtypeStruct((ROWS, D), b...  120 us
    pallas_call x1, Pallas kernels, back(): pl.pallas_call(back_kernel, out_shape=(jax.ShapeDtypeStruct((TOTAL, F), f...  74.4 us
    pallas_call x1, Pallas kernels, weight_grads(): pl.pallas_call(weight_kernel, grid=(steps,), out_shape=[jax.ShapeDtypeStr...  14.6 us
    pallas_call x1, Pallas kernels, own_back(): pl.pallas_call(own_back_kernel, grid=(2,), out_shape=jax.ShapeDtypeStruct...  6.62 us

profile of v1, /device:TPU:1, one launch (start us, length us, event | category | flops | bytes accessed | tf_op | source)
XLA Modules:
  0.0 216.6 jit_solution(15454793535059678614)
XLA Ops:
  0.6 119.7 %front.1 = (bf16[64,3072]{1,0:T(8,128)(2,1)}, bf16[64,3072]{1,0:T(8,128)(2,1)}, f32[512,1152]{1,0:T(8,128)}, bf16[3072,512]{1,0:T(8,128)(2,1)}, bf16[384,512]{1,...) custom-call(bf16[64,3072]{1,0:T(8,128)(2,1)} %bitcast.14, ...), custom_call_target="tpu_custom_call" | custom-call | tf_op jit(solution)/shard_map/front/pallas_call | solution.py:579
  120.4 74.4 %back.1 = (f32[512,384]{1,0:T(8,128)}, bf16[384,3072]{1,0:T(8,128)(2,1)}, bf16[3,3072,384]{2,1,0:T(8,128)(2,1)}) custom-call(bf16[3,512,384]{2,1,0:T(8,128)(2,1)} %get-tuple-element.25.grad_ref, bf16[64,3072]{1,0:T(8,128)(2,1)} %get-tuple-element.26.rows_ref, f32[1,3072]{1,0:T(1,128)} %gain_ref.3, f32[8,3072]{1,0:T(8,128)} %get-tuple-element.27.image_ref, ...), custom_call_target="tpu_custom_call" | custom-call | tf_op jit(solution)/shard_map/back/pallas_call | solution.py:784
  194.8 6.6 %own_back.1.grad_ref = bf16[3,512,384]{2,1,0:T(8,128)(2,1)} custom-call(f32[512,1152]{1,0:T(8,128)} %get-tuple-element.24.proj_ref, f32[2,128]{1,0:T(2,128)} %bitcast.16, f32[512,384]{1,0:T(8,128)} %get-tuple-element.31.grad_ref), custom_call_target="tpu_custom_call" | custom-call | tf_op jit(solution)/shard_map/own_back/pallas_call | solution.py:829
  201.4 0.0 copy-start
  201.4 14.6 %weight_grads.1 = (bf16[3,3072,384]{2,1,0:T(8,128)(2,1)}, bf16[64,3072]{1,0:T(8,128)(2,1)}, bf16[384,3072]{1,0:T(8,128)(2,1)}, bf16[384,512]{1,0:T(8,128)(2,1)}) custom-call(bf16[3072,512]{1,0:T(8,128)(2,1)} %get-tuple-element.23.turned_ref, bf16[3,512,384]{2,1,0:T(8,128)(2,1)} %own_back.1.grad_ref, bf16[3,3072,384]{2,1,0:T(8,128)(2,1)} %get-tuple-element.32.part_ref, ...), custom_call_target="tpu_custom_call" | custom-call | tf_op jit(solution)/shard_map/weight_grads/pallas_call | solution.py:862
  216.0 0.0 copy-done
  216.0 0.5 copy.14
Async XLA Ops:
  201.4 14.6 %copy-start = (f32[1,2]{1,0:T(1,128)S(1)}, f32[1,2]{1,0:T(1,128)}, u32[]{:S(2)}) copy-start(f32[1,2]{1,0:T(1,128)} %get-tuple-element.50) | copy-start | bytes 28

commit v2 on v1

v2 whole, which is shorter than its diff:
```python
import functools
import math

import jax
import jax.numpy as jnp
from jax import lax
from jax.experimental import pallas as pl
from jax.experimental.pallas import tpu as pltpu
from jax.sharding import PartitionSpec as P

HS = 128
PATCHES = 256
EPS = 1e-06
N_DP = 4
N_T = 2
ROWS = 64
TOTAL = 512
D = 3072
F = 384
TALL = 512
STEPS = D // TALL
CLASSES = 512
PROJECT_PLAN = (('A', 768, (1, 1)), ('B', 1024, (-1,)), ('A', 256, (1, -1)), ('B', 256, (-1,)), ('B', 256, (1,)), ('A', 512, (-1, -1)))
PROJECT_STEPS = (
    (1, 0, 0, 0, 1), (1, 1, 0, 3, 0), (1, -1, 0, 1, 0), (1, 0, 1, 0, 1), (1, 1, 1, 3, 0), (1, -1, 1, 1, 0),
    (0, 0, 3, 0), (1, 1, 0, 2, 0), (0, 0, 1, 0), (1, 0, 2, 0, 1), (1, -1, 2, 1, 0), (0, 0, 0, 1),
    (1, 1, 0, 3, 1), (1, -1, 0, 1, 1), (1, 0, 3, 0, 1), (1, 0, 4, 0, 1), (1, 0, 5, 0, 1), (0, 1, 3, 0),
    (1, 0, 1, 3, 1), (0, 1, 1, 0), (1, -1, 1, 2, 0), (1, 0, 1, 1, 1), (0, 2, 1, 0), (0, 1, 0, 1),
    (0, 2, 0, 1), (1, 1, 2, 3, 1), (1, -1, 2, 1, 1), (0, 0, 2, 0), (0, 3, 0, 1), (1, 1, 2, 3, 0),
    (0, 0, 1, 1), (0, 4, 0, 1), (1, 1, 3, 3, 0), (1, 1, 4, 3, 0), (1, -1, 3, 1, 0), (0, 0, 3, 1),
    (1, 1, 0, 2, 1), (0, 5, 0, 1), (1, 1, 5, 3, 1), (1, -1, 5, 1, 1), (0, 2, 3, 1), (0, 2, 3, 0),
    (1, 1, 2, 2, 0), (0, 1, 2, 0), (1, 0, 1, 2, 1), (1, -1, 4, 1, 0), (0, 3, 3, 0), (1, 0, 3, 3, 1),
    (0, 2, 1, 1), (1, -1, 2, 2, 1), (0, 4, 3, 0), (1, 1, 4, 2, 0), (1, 0, 4, 3, 1), (0, 3, 1, 0),
    (1, -1, 3, 2, 0), (1, 0, 3, 1, 1), (0, 1, 3, 1), (1, -1, 5, 1, 0), (0, 5, 1, 1), (1, -1, 5, 2, 1),
    (0, 0, 2, 1), (2, 0, 0), (0, 4, 1, 0), (1, 0, 4, 1, 1), (0, 2, 2, 1), (0, 1, 1, 1),
    (1, 1, 5, 3, 0), (2, 0, 1), (0, 5, 3, 1), (0, 3, 2, 0), (1, 0, 3, 2, 1), (0, 2, 2, 0),
    (2, 2, 0), (2, 2, 1), (0, 4, 2, 0), (1, 0, 4, 2, 1), (0, 5, 1, 0), (1, -1, 5, 2, 0),
    (0, 1, 2, 1), (2, 1, 0), (0, 5, 3, 0), (0, 5, 2, 1), (0, 3, 3, 1), (2, 1, 1),
    (0, 4, 3, 1), (0, 3, 1, 1), (0, 5, 2, 0), (2, 5, 0), (0, 4, 1, 1), (2, 5, 1),
    (0, 3, 2, 1), (2, 3, 0), (2, 3, 1), (0, 4, 2, 1), (2, 4, 0), (2, 4, 1),
)
RETURN_PLAN = (('B', 256, (-1,)), ('B', 256, (1,)), ('A', 1024, (-1, 1)), ('B', 256, (-1,)), ('A', 768, (-1, 1)), ('B', 512, (1,)))
RETURN_STEPS = (
    (1, 1, 0, 3, 0), (1, -1, 0, 1, 0), (1, 0, 0, 0, 1), (1, 1, 1, 3, 0), (1, -1, 1, 1, 0), (1, 0, 1, 0, 1),
    (1, 0, 2, 0, 1), (1, 1, 2, 3, 0), (1, -1, 2, 1, 0), (1, 1, 3, 3, 0), (1, -1, 3, 1, 0), (1, 0, 3, 0, 1),
    (1, 0, 4, 0, 1), (1, 1, 4, 3, 0), (1, -1, 4, 1, 0), (3, 0), (3, 1), (0, 0, 3, 0),
    (1, 0, 0, 3, 1), (0, 0, 1, 0), (1, -1, 0, 2, 0), (1, 0, 0, 1, 1), (1, 1, 5, 3, 0), (1, -1, 5, 1, 0),
    (3, 2), (0, 1, 3, 0), (1, 1, 1, 2, 0), (1, 0, 1, 3, 1), (0, 1, 1, 0), (1, 0, 1, 1, 1),
    (0, 0, 0, 1), (3, 3), (0, 1, 0, 1), (3, 4), (1, 0, 5, 0, 1), (3, 5),
    (0, 2, 3, 0), (0, 2, 1, 0), (1, -1, 2, 2, 0), (3, 6), (0, 3, 3, 0), (1, 0, 3, 3, 1),
    (0, 3, 1, 0), (1, -1, 3, 2, 0), (1, 0, 3, 1, 1), (0, 2, 0, 1), (1, 1, 2, 3, 1), (1, -1, 2, 1, 1),
    (3, 7), (0, 3, 0, 1), (0, 4, 3, 0), (0, 4, 1, 0), (1, -1, 4, 2, 0), (0, 0, 2, 0),
    (1, 0, 0, 2, 1), (0, 4, 0, 1), (1, 1, 4, 3, 1), (1, -1, 4, 1, 1), (0, 5, 3, 0), (1, 1, 5, 2, 0),
    (1, 0, 5, 3, 1), (0, 0, 3, 1), (0, 1, 2, 0), (1, 0, 1, 2, 1), (0, 5, 1, 0), (1, 0, 5, 1, 1),
    (0, 0, 1, 1), (0, 1, 3, 1), (0, 1, 1, 1), (0, 2, 3, 1), (1, 1, 2, 2, 1), (0, 2, 2, 0),
    (0, 5, 0, 1), (0, 3, 2, 0), (1, 0, 3, 2, 1), (0, 3, 3, 1), (0, 3, 1, 1), (0, 4, 3, 1),
    (1, 1, 4, 2, 1), (0, 0, 2, 1), (2, 0, 0), (2, 0, 1), (0, 5, 2, 0), (1, 0, 5, 2, 1),
    (0, 2, 1, 1), (0, 5, 3, 1), (0, 1, 2, 1), (2, 1, 0), (2, 1, 1), (0, 4, 2, 0),
    (0, 5, 1, 1), (0, 2, 2, 1), (2, 2, 0), (0, 3, 2, 1), (2, 2, 1), (2, 3, 0),
    (0, 4, 1, 1), (2, 3, 1), (0, 5, 2, 1), (2, 5, 0), (2, 5, 1), (0, 4, 2, 1),
    (2, 4, 0), (2, 4, 1),
)
OUT_PLAN = (('A', 512, (1, 1)), ('A', 256, (1, 1)), ('B', 1280, (-1,)), ('A', 512, (-1, 1)), ('A', 512, (1, -1)))
OUT_STEPS = (
    (0, 0), (1, 0, 1, 0), (1, 0, 1, 1), (1, 0, -1, 2), (1, 0, -1, 3), (0, 1),
    (0, 2), (1, 2, 0, 0), (0, 3), (1, 1, 1, 0), (1, 1, -1, 2), (0, 4),
    (1, 1, 1, 1), (1, 1, -1, 3), (1, 3, 1, 1), (1, 2, 0, 1), (1, 3, -1, 0), (2, 0, (0,), 1, 4),
    (1, 3, -1, 3), (2, 0, (1,), 1, 5), (1, 4, -1, 1), (2, 1, (0,), 1, 4), (1, 2, 0, 2), (2, 1, (1,), 1, 5),
    (1, 4, -1, 2), (2, 2, (0,), -1, 4), (2, 3, (1,), 1, 5), (2, 3, (0,), -1, 4), (1, 3, 1, 2), (1, 2, 0, 3),
    (2, 0, (3, 5), 0, 6), (2, 4, (1,), -1, 5), (1, 4, 1, 0), (2, 1, (3, 5), 0, 6), (1, 4, 1, 3), (2, 3, (3, 5), 0, 6),
    (2, 2, (2,), 1, 5), (2, 2, (1, 4), -1, 6), (2, 4, (0,), 1, 4), (2, 4, (3, 5), 0, 6), (2, 0, (2, 4, 6), None, None), (2, 1, (2, 4, 6), None, None),
    (2, 3, (2, 4, 6), None, None), (2, 2, (3, 5, 6), None, None), (2, 4, (2, 4, 6), None, None),
)
INPUT_PLAN = (('B', 256, (-1,)), ('A', 768, (-1, 1)), ('B', 256, (1,)), ('B', 1024, (1,)), ('A', 512, (1, -1)), ('A', 256, (-1, -1)))
INPUT_STEPS = (
    (0, 0), (1, 0, 0, 0), (1, 0, 0, 1), (1, 0, 0, 2), (1, 0, 0, 3), (0, 1),
    (1, 1, -1, 0), (1, 1, 1, 1), (1, 1, 1, 2), (1, 1, -1, 3), (0, 2), (1, 2, 0, 0),
    (1, 2, 0, 1), (1, 2, 0, 2), (1, 2, 0, 3), (0, 3), (2, 0, (0,), -1, 4), (2, 0, (2,), 1, 5),
    (1, 3, 0, 0), (1, 3, 0, 1), (1, 3, 0, 2), (1, 3, 0, 3), (0, 4), (2, 1, (0,), -1, 4),
    (2, 1, (1,), 1, 5), (2, 2, (0,), 1, 4), (1, 4, 1, 0), (1, 4, -1, 1), (1, 4, -1, 2), (1, 4, 1, 3),
    (0, 5), (2, 2, (2,), -1, 5), (1, 5, -1, 0), (1, 5, -1, 1), (1, 5, 1, 2), (1, 5, 1, 3),
    (2, 0, (1, 4), -1, 6), (2, 3, (0,), 1, 4), (2, 1, (3, 5), 0, 6), (2, 2, (1, 4), 1, 6), (2, 4, (1,), -1, 5), (2, 4, (0,), 1, 4),
    (2, 5, (0,), -1, 4), (2, 5, (1,), -1, 5), (2, 0, (3, 5, 6), None, None), (2, 3, (2,), -1, 5), (2, 4, (3, 5), 0, 6), (2, 3, (1, 4), 1, 6),
    (2, 5, (3, 5), 0, 6), (2, 2, (3, 5, 6), None, None), (2, 1, (2, 4, 6), None, None), (2, 4, (2, 4, 6), None, None), (2, 5, (2, 4, 6), None, None), (2, 3, (3, 5, 6), None, None),
)
MESH = pl.DeviceIdType.MESH
f32 = jnp.float32
bf16 = jnp.bfloat16
VM = pl.BlockSpec(memory_space=pltpu.VMEM)
ANY = pl.BlockSpec(memory_space=pl.ANY)


def dot_nn(a, b):
    return lax.dot_general(a, b, (((1,), (0,)), ((), ())), preferred_element_type=f32)


def dot_nt(a, b):
    return lax.dot_general(a, b, (((1,), (1,)), ((), ())), preferred_element_type=f32)


def norm_last(values, gain_row):
    centered = values - jnp.mean(values, axis=-1, keepdims=True)
    inverse = lax.rsqrt(jnp.mean(centered * centered, axis=-1, keepdims=True) + EPS)
    unit_rows = centered * inverse
    return unit_rows * gain_row, unit_rows, inverse


def norm_back(grad, unit_rows, inverse, gain_row):
    scaled = grad * gain_row
    return inverse * (
        scaled
        - jnp.mean(scaled, axis=-1, keepdims=True)
        - unit_rows * jnp.mean(scaled * unit_rows, axis=-1, keepdims=True)
    )


def place():
    return lax.axis_index("dp"), lax.axis_index("tensor")


def neighbour(dz, dt):
    z, t = place()
    target = {}
    if dz:
        target["dp"] = lax.rem(z + dz + N_DP, N_DP)
    if dt:
        target["tensor"] = 1 - t
    return target


def section_at(step):
    s, n = lax.axis_index("section"), lax.axis_size("section")
    return {"section": lax.rem(s + step + n, n)}


def greet(devices):
    barrier = pltpu.get_barrier_semaphore()
    for device in devices:
        pl.semaphore_signal(barrier, inc=1, device_id=device, device_id_type=MESH)


def enter(devices):
    pl.semaphore_wait(pltpu.get_barrier_semaphore(), len(devices))


def rows_of(dz, dt):
    z, t = place()
    owner = lax.rem(z + dz + N_DP, N_DP) * N_T + ((1 - t) if dt else t)
    return pl.ds(pl.multiple_of(owner * ROWS, ROWS), ROWS)


class Plan:
    def __init__(self, plan):
        self.kinds = [kind for kind, _, _ in plan]
        self.widths = [width for _, width, _ in plan]
        self.ways = [ways for _, _, ways in plan]
        self.count = len(plan)
        self.sent = []

    def columns(self, c):
        return pl.ds(sum(self.widths[:c]), self.widths[c])

    def finish(self):
        for copy in self.sent:
            copy.wait_send()


class Gather(Plan):
    def __init__(self, plan, buf, send_sem, recv_sem):
        super().__init__(plan)
        self.buf, self.send_sem, self.recv_sem = buf, send_sem, recv_sem

    def copy(self, c, dz, dt, slot, device):
        part = self.buf.at[rows_of(dz, dt), self.columns(c)]
        return pltpu.make_async_remote_copy(
            src_ref=part,
            dst_ref=part,
            send_sem=self.send_sem.at[c, slot],
            recv_sem=self.recv_sem.at[c, slot],
            device_id=device,
            device_id_type=MESH,
        )

    def run(self, steps, compute, side=None, prepare=None):
        ready, begun = set(), set()
        for kind, *step in steps:
            if kind == 0:
                c, dz, dt = step
                self.copy(c, dz, dt, dz * 2 + dt, neighbour(1, 0)).wait_recv()
            elif kind == 1:
                way, c, dz, dt = step
                from_z, from_t = (dz + way) % N_DP, dt if way else 1 - dt
                if (from_z, from_t) == (0, 0) and c not in ready:
                    ready.add(c)
                    if prepare is not None:
                        prepare(c)
                device = neighbour(way, 0) if way else neighbour(0, 1)
                copy = self.copy(c, from_z, from_t, dz * 2 + dt, device)
                copy.start()
                self.sent.append(copy)
            elif kind == 2:
                c, r = step
                compute(c, r, r not in begun)
                begun.add(r)
            else:
                side(step[0])


RING = ((1, 0), (-1, 0), (0, 1))


class Scatter(Plan):
    def __init__(self, plan, part, land, send_sem, recv_sem):
        super().__init__(plan)
        self.part, self.land = part, land
        self.send_sem, self.recv_sem = send_sem, recv_sem

    def view(self, dz, dt, c):
        return self.part.at[rows_of(dz, dt), self.columns(c)]

    def copy(self, c, dz, dt, slot, device):
        return pltpu.make_async_remote_copy(
            src_ref=self.view(dz, dt, c),
            dst_ref=self.land.at[slot, :, self.columns(c)],
            send_sem=self.send_sem.at[c, slot],
            recv_sem=self.recv_sem.at[c, slot],
            device_id=device,
            device_id_type=MESH,
        )

    def send(self, c, dz, dt, way, slot):
        device = neighbour(way, 0) if way else neighbour(0, 1)
        copy = self.copy(c, dz, dt, slot, device)
        copy.start()
        self.sent.append(copy)

    def block(self, c, slot):
        first, last = self.ways[c][0], self.ways[c][-1]
        if self.kinds[c] == "A":
            names = ((2, 0), (2, 1), (-first, 0), (-last, 1), (first, 0), (last, 1), (0, 1))
        else:
            names = ((2, 1), (first, 1), (-first, 1), (0, 1), (2, 0), (-first, 0), (first, 0))
        return names[slot]

    def run(self, steps, compute, done):
        for kind, c, *step in steps:
            if kind == 0:
                compute(c)
            elif kind == 1:
                way, slot = step
                self.send(c, *self.block(c, slot), way, slot)
            else:
                slots, way, slot = step
                dz, dt = (0, 0) if way is None else self.block(c, slot)
                rows = rows_of(dz, dt)
                total = self.part[rows, self.columns(c)].astype(f32)
                for came in slots:
                    self.copy(c, 0, 0, came, neighbour(1, 0)).wait_recv()
                    total = total + self.land[came, :, self.columns(c)].astype(f32)
                if way is None:
                    done(c, total)
                else:
                    self.part[rows, self.columns(c)] = total.astype(bf16)
                    self.send(c, dz, dt, way, slot)


def params(collective_id=None, limit=62 * 1024 * 1024):
    if collective_id is None:
        return pltpu.CompilerParams(vmem_limit_bytes=limit)
    return pltpu.CompilerParams(
        collective_id=collective_id, has_side_effects=True, vmem_limit_bytes=limit
    )


def ring_sems(plan):
    return [pltpu.SemaphoreType.DMA((len(plan), 8)), pltpu.SemaphoreType.DMA((len(plan), 8))]


def land_scratch():
    return [pltpu.VMEM((TOTAL, D), bf16), pltpu.VMEM((7, ROWS, D), bf16)]


def image_rows(i):
    return pl.ds(pl.multiple_of(i * PATCHES, PATCHES), PATCHES)


def project_chunk(buf, wbuf, proj, turned, first, cols, r):
    rows = pl.ds(r * PATCHES, PATCHES)
    block = buf[rows, cols]
    value = dot_nn(block, wbuf[cols, :])
    if first:
        proj[rows, :] = value
    else:
        proj[rows, :] += value
    turned[cols, rows] = block.T


def side_by_side(w_hbm, wbuf, sems):
    return [
        pltpu.make_async_copy(w_hbm.at[t], wbuf.at[:, pl.ds(t * F, F)], sems.at[t])
        for t in range(3)
    ]


def head_cols(t, h):
    return pl.ds(t * F + h * HS, HS)


def head_state(q, k, v, pair):
    q_normed, q_unit, q_inv = norm_last(q, pair[0:1, :])
    k_normed, k_unit, k_inv = norm_last(k, pair[1:2, :])
    q_half, k_half = q_normed.astype(bf16), k_normed.astype(bf16)
    v_half = v.astype(bf16)
    exponent = jnp.exp(dot_nt(q_half, k_half) * (1.0 / math.sqrt(HS)))
    probs = exponent * (1.0 / jnp.sum(exponent, axis=-1, keepdims=True))
    return q_unit, q_inv, k_unit, k_inv, q_half, k_half, v_half, probs


def state_of(proj, pair, rows, h):
    return head_state(*[proj[rows, head_cols(t, h)] for t in range(3)], pair)


def attend(proj, pair_ref, att, turned):
    def image(i, carry):
        rows = image_rows(i)
        for h in range(3):
            v_half, probs = state_of(proj, pair_ref[...], rows, h)[-2:]
            mixed = dot_nn(probs.astype(bf16), v_half)
            att[rows, pl.ds(h * HS, HS)] = mixed.astype(bf16)
            if turned is not None:
                turned[pl.ds(h * HS, HS), rows] = mixed.T.astype(bf16)
        return carry

    lax.fori_loop(0, 2, image, 0)


def keep_scratch():
    return [
        pltpu.VMEM((6, PATCHES, PATCHES), f32),
        pltpu.VMEM((6, PATCHES, PATCHES), bf16),
        pltpu.VMEM((TOTAL, 3 * F), bf16),
        pltpu.VMEM((TOTAL, 2 * F), f32),
        pltpu.VMEM((12, PATCHES, 1), f32),
    ]


def keep_image(proj, pair_ref, kept, i, sums=None):
    probs_ref, turned_ref, halves_ref, unit_ref, inv_ref = kept
    rows = image_rows(i)
    for h in range(3):
        q_unit, q_inv, k_unit, k_inv, q_half, k_half, v_half, probs = state_of(
            proj, pair_ref[...], rows, h
        )
        slot = i * 3 + h
        probs_ref[slot] = probs
        turned_ref[slot] = probs.T.astype(bf16)
        for t, value in enumerate((q_half, k_half, v_half)):
            halves_ref[rows, head_cols(t, h)] = value
        unit_ref[rows, head_cols(0, h)] = q_unit
        unit_ref[rows, head_cols(1, h)] = k_unit
        inv_ref[2 * slot] = q_inv
        inv_ref[2 * slot + 1] = k_inv
        if sums is not None:
            mixed = dot_nn(probs.astype(bf16), v_half).astype(bf16).astype(f32)
            row_id = lax.broadcasted_iota(jnp.int32, (8, 1), 0)
            total = jnp.sum(mixed, axis=0, keepdims=True)
            sums[:, pl.ds(h * HS, HS)] += jnp.where(row_id == i, total, 0.0)


def back_image(kept, pair_ref, mixed_of, out, i):
    probs_ref, turned_ref, halves_ref, unit_ref, inv_ref = kept
    rows = image_rows(i)
    pair = pair_ref[...]
    for h in range(3):
        slot = i * 3 + h
        probs = probs_ref[slot]
        q_half, k_half, v_half = [halves_ref[rows, head_cols(t, h)] for t in range(3)]
        mixed = mixed_of(i, rows, h)
        grad_probs = dot_nt(mixed, v_half)
        grad_value = dot_nn(turned_ref[slot], mixed)
        grad_scores = probs * (grad_probs - jnp.sum(probs * grad_probs, axis=-1, keepdims=True))
        scaled = grad_scores * (1.0 / math.sqrt(HS))
        grad_query = dot_nn(scaled.astype(bf16), k_half)
        grad_key = dot_nn(scaled.T.astype(bf16), q_half)
        q_unit, k_unit = [unit_ref[rows, head_cols(t, h)] for t in range(2)]
        back_q = norm_back(grad_query, q_unit, inv_ref[2 * slot], pair[0:1, :])
        back_k = norm_back(grad_key, k_unit, inv_ref[2 * slot + 1], pair[1:2, :])
        for t, value in enumerate((back_q, back_k, grad_value)):
            out[rows, head_cols(t, h)] = value.astype(bf16)


def both_images(step):
    def body(i, carry):
        step(i)
        return carry

    lax.fori_loop(0, 2, body, 0)


PEERS = tuple((dz, dt) for dz in range(N_DP) for dt in range(N_T) if dz or dt)
PACK = D // 4


def front_kernel(
    rows_ref,
    gain_ref,
    pair_ref,
    pool_ref,
    label_ref,
    w_hbm,
    wout_hbm,
    head_hbm,
    out_ref,
    margin_ref,
    proj_hbm,
    turned_hbm,
    att_turned_ref,
    margin_turned_hbm,
    margin_grad_ref,
    head_grad_ref,
    image_ref,
    sums_ref,
    loss_ref,
    wbuf,
    wout,
    head,
    buf_own,
    buf_margin,
    proj_own,
    proj_margin,
    turned_own,
    turned_margin,
    att,
    part,
    land,
    next_rows,
    stage,
    pool_land,
    pooled_ref,
    half_ref,
    per_image,
    *rest,
):
    kept = rest[:5]
    (
    load_sem,
    store_sem,
    own_send,
    own_recv,
    sum_send,
    sum_recv,
    step_send,
    step_recv,
    margin_send,
    margin_recv,
    pool_send,
    pool_recv,
    ) = rest[5:]
    load_w = side_by_side(w_hbm, wbuf, load_sem)
    load_out = pltpu.make_async_copy(wout_hbm, wout, load_sem.at[3])
    load_head = pltpu.make_async_copy(head_hbm, head, load_sem.at[4])
    for load in load_w:
        load.start()
    load_out.start()
    load_head.start()
    devices = [neighbour(*way) for way in PEERS] + [section_at(1), section_at(-1)]
    greet(devices)
    normed, _, _ = norm_last(rows_ref[...].astype(f32), gain_ref[...])
    buf_own[rows_of(0, 0), :] = normed.astype(bf16)
    enter(devices)

    gather = Gather(PROJECT_PLAN, buf_own, own_send, own_recv)

    waiting = list(load_w)

    def compute_own(c, r, first):
        while waiting:
            waiting.pop().wait()
        project_chunk(buf_own, wbuf, proj_own, turned_own, first, gather.columns(c), r)

    gather.run(PROJECT_STEPS, compute_own)
    stores = [
        pltpu.make_async_copy(proj_own, proj_hbm, store_sem.at[0]),
        pltpu.make_async_copy(turned_own, turned_hbm, store_sem.at[1]),
    ]
    for store in stores:
        store.start()
    attend(proj_own, pair_ref, att, att_turned_ref)

    load_out.wait()
    scatter = Scatter(OUT_PLAN, part, land, sum_send, sum_recv)
    hops = []

    def out_chunk(c):
        cols = scatter.columns(c)

        def tile(r, carry):
            rows = image_rows(r)
            part[rows, cols] = dot_nn(att[rows, :], wout[:, cols]).astype(bf16)
            return carry

        lax.fori_loop(0, TOTAL // PATCHES, tile, 0)

    def out_done(c, total):
        cols = scatter.columns(c)
        out_ref[:, cols] = (rows_ref[:, cols].astype(f32) + total).astype(bf16)
        copy = pltpu.make_async_remote_copy(
            src_ref=out_ref.at[:, cols],
            dst_ref=next_rows.at[:, cols],
            send_sem=step_send.at[c],
            recv_sem=step_recv.at[c],
            device_id=section_at(1),
            device_id_type=MESH,
        )
        copy.start()
        hops.append(copy)

    scatter.run(OUT_STEPS, out_chunk, out_done)
    for copy in hops:
        copy.wait_recv()
    first = lax.axis_index("section") == 0
    margin = jnp.where(first, rows_ref[...], next_rows[...])
    margin_ref[...] = margin
    normed, _, _ = norm_last(margin.astype(f32), gain_ref[...])
    buf_margin[rows_of(0, 0), :] = normed.astype(bf16)
    second = Gather(PROJECT_PLAN, buf_margin, margin_send, margin_recv)
    second.run(
        PROJECT_STEPS,
        lambda c, r, first: project_chunk(
            buf_margin, wbuf, proj_margin, turned_margin, first, second.columns(c), r
        ),
    )
    store = pltpu.make_async_copy(turned_margin, margin_turned_hbm, store_sem.at[2])
    store.start()
    stores.append(store)
    sums_ref[...] = jnp.zeros_like(sums_ref)
    both_images(lambda i: keep_image(proj_margin, pair_ref, kept, i, sums_ref))

    row_id = lax.broadcasted_iota(jnp.int32, (8, 1), 0)
    sums = sums_ref[...]
    hi = sums.astype(bf16).astype(f32)
    mid = (sums - hi).astype(bf16).astype(f32)
    low = sums - hi - mid
    tall = jnp.concatenate([hi, mid, low], axis=0).astype(bf16)
    terms = dot_nn(tall, wout[...])
    partial_rows = terms[0:8] + terms[8:16] + terms[16:24]
    own = jnp.sum(margin_ref[...].astype(f32), axis=0, keepdims=True)
    image = lax.axis_index("dp") // (N_DP // 2)
    partial_rows = partial_rows + jnp.where(row_id == image, own, 0.0)
    for i in range(2):
        for q in range(4):
            stage[i * 4 + q : i * 4 + q + 1, :] = partial_rows[i : i + 1, q * PACK : (q + 1) * PACK]
    copies = []
    for k, way in enumerate(PEERS):
        copy = pltpu.make_async_remote_copy(
            src_ref=stage,
            dst_ref=pool_land.at[k],
            send_sem=pool_send.at[k],
            recv_sem=pool_recv.at[k],
            device_id=neighbour(*way),
            device_id_type=MESH,
        )
        copy.start()
        copies.append(copy)
    load_head.wait()
    total = stage[...]
    for k, copy in enumerate(copies):
        copy.wait_recv()
        total = total + pool_land[k]
    pooled_ref[...] = jnp.zeros_like(pooled_ref)
    for i in range(2):
        for q in range(4):
            pooled_ref[i : i + 1, q * PACK : (q + 1) * PACK] = total[i * 4 + q : i * 4 + q + 1, :]
    gain = pool_ref[...]
    normed, unit_rows, inverse = norm_last(pooled_ref[...] / PATCHES, gain)
    half = normed.astype(bf16)
    half_ref[...] = half.astype(f32)
    logits = dot_nn(half, head[...])
    label = jnp.where(row_id == 0, label_ref[0:1, 0:1], label_ref[0:1, 1:2])
    targets = (label == lax.broadcasted_iota(jnp.int32, (8, CLASSES), 1)).astype(f32)
    soft = jnp.maximum(logits, 0.0) + jnp.log1p(jnp.exp(-jnp.abs(logits)))
    loss = jnp.mean(soft - targets * logits, axis=-1, keepdims=True)
    lane = lax.broadcasted_iota(jnp.int32, (8, 128), 1)
    loss_ref[...] = jnp.sum(jnp.where(row_id == lane, loss, 0.0), axis=0, keepdims=True)[:, 0:2]
    grad_logits = (jax.nn.sigmoid(logits) - targets) / 2
    grad_logits = jnp.where(row_id < 2, grad_logits, 0.0).astype(bf16)
    grad_pooled = norm_back(dot_nt(grad_logits, head[...]), unit_rows, inverse, gain)
    grad_image = grad_pooled / PATCHES
    image_ref[...] = jnp.where(row_id < 2, grad_image, 0.0)
    per_image[...] = dot_nt(grad_image.astype(bf16), wout[...])
    z, t = place()
    width = D // (N_DP * N_T)
    start = pl.multiple_of((z * N_T + t) * width, width)
    mine = half_ref[:, pl.ds(start, width)]
    head_grad_ref[...] = dot_nn(mine.T.astype(bf16), grad_logits).astype(bf16)

    def shared_cotangent(i, rows, h):
        cols = pl.ds(h * HS, HS)
        row = jnp.where(i == 0, per_image[0:1, cols], per_image[1:2, cols])
        return jnp.broadcast_to(row, (PATCHES, HS)).astype(bf16)

    both_images(lambda i: back_image(kept, pair_ref, shared_cotangent, margin_grad_ref, i))
    gather.finish()
    scatter.finish()
    second.finish()
    for copy in hops + copies:
        copy.wait_send()
    for store in stores:
        store.wait()


def front(rows, gain_row, gain_pair, pool_row, labels, qkv_local, out_local, head_local, collective_id):
    return pl.pallas_call(
        front_kernel,
        out_shape=(
            jax.ShapeDtypeStruct((ROWS, D), bf16),
            jax.ShapeDtypeStruct((ROWS, D), bf16),
            jax.ShapeDtypeStruct((TOTAL, 3 * F), f32),
            jax.ShapeDtypeStruct((D, TOTAL), bf16),
            jax.ShapeDtypeStruct((F, TOTAL), bf16),
            jax.ShapeDtypeStruct((D, TOTAL), bf16),
            jax.ShapeDtypeStruct((TOTAL, 3 * F), bf16),
            jax.ShapeDtypeStruct((F, CLASSES), bf16),
            jax.ShapeDtypeStruct((8, D), f32),
            jax.ShapeDtypeStruct((8, F), f32),
            jax.ShapeDtypeStruct((1, 2), f32),
        ),
        in_specs=[VM, VM, VM, VM, VM, ANY, ANY, ANY],
        out_specs=(VM, VM, ANY, ANY, VM, ANY, VM, VM, VM, VM, VM),
        scratch_shapes=[
            pltpu.VMEM((D, 3 * F), bf16),
            pltpu.VMEM((F, D), bf16),
            pltpu.VMEM((D, CLASSES), bf16),
            pltpu.VMEM((TOTAL, D), bf16),
            pltpu.VMEM((TOTAL, D), bf16),
            pltpu.VMEM((TOTAL, 3 * F), f32),
            pltpu.VMEM((TOTAL, 3 * F), f32),
            pltpu.VMEM((D, TOTAL), bf16),
            pltpu.VMEM((D, TOTAL), bf16),
            pltpu.VMEM((TOTAL, F), bf16),
        ]
        + land_scratch()
        + [
            pltpu.VMEM((ROWS, D), bf16),
            pltpu.VMEM((8, PACK), f32),
            pltpu.VMEM((len(PEERS), 8, PACK), f32),
            pltpu.VMEM((8, D), f32),
            pltpu.VMEM((8, D), f32),
            pltpu.VMEM((8, F), f32),
        ]
        + keep_scratch()
        + [
            pltpu.SemaphoreType.DMA((5,)),
            pltpu.SemaphoreType.DMA((3,)),
        ]
        + ring_sems(PROJECT_PLAN)
        + ring_sems(OUT_PLAN)
        + [pltpu.SemaphoreType.DMA((len(OUT_PLAN),))] * 2
        + ring_sems(PROJECT_PLAN)
        + [pltpu.SemaphoreType.DMA((len(PEERS),)), pltpu.SemaphoreType.DMA((len(PEERS),))],
        compiler_params=params(collective_id),
        name="front",
    )(rows, gain_row, gain_pair, pool_row, labels, qkv_local, out_local, head_local)


def back_kernel(
    grad_ref,
    rows_ref,
    gain_ref,
    pair_ref,
    image_ref,
    sums_ref,
    w_hbm,
    wout_hbm,
    turned_hbm,
    margin_turned_hbm,
    proj_hbm,
    own_grad_ref,
    grad_out_hbm,
    margin_part_hbm,
    part,
    land,
    wbuf,
    wout,
    turned,
    margin_turned,
    total_ref,
    mine,
    came,
    buf,
    grad_out,
    margin_part,
    proj,
    grad_att_ref,
    *rest,
):
    kept = rest[:5]
    (
    wsem,
    load_sem,
    out_sem,
    part_sem,
    sum_send,
    sum_recv,
    step_send,
    step_recv,
    own_send,
    own_recv,
    ) = rest[5:]
    devices = [neighbour(*way) for way in RING] + [section_at(1), section_at(-1)]
    greet(devices)
    scatter = Scatter(INPUT_PLAN, part, land, sum_send, sum_recv)
    loads = []
    for c in range(scatter.count):
        for t in range(3):
            load = pltpu.make_async_copy(
                w_hbm.at[t, scatter.columns(c), :],
                wbuf.at[scatter.columns(c), pl.ds(t * F, F)],
                wsem.at[3 * c + t],
            )
            load.start()
            loads.append(load)
    later = [
        pltpu.make_async_copy(margin_turned_hbm, margin_turned, load_sem.at[0]),
        pltpu.make_async_copy(wout_hbm, wout, load_sem.at[1]),
        pltpu.make_async_copy(turned_hbm, turned, load_sem.at[2]),
        pltpu.make_async_copy(proj_hbm, proj, load_sem.at[3]),
    ]
    for load in later:
        load.start()
    enter(devices)

    def compute(c):
        for load in loads[3 * c : 3 * c + 3]:
            load.wait()
        cols = scatter.columns(c)

        def tile(r, carry):
            rows = image_rows(r)
            part[rows, cols] = dot_nt(grad_ref[rows, :], wbuf[cols, :]).astype(bf16)
            return carry

        lax.fori_loop(0, TOTAL // PATCHES, tile, 0)

    def done(c, total):
        total_ref[:, scatter.columns(c)] = total

    scatter.run(INPUT_STEPS, compute, done)
    gain = gain_ref[...]
    _, unit_rows, inverse = norm_last(rows_ref[...].astype(f32), gain)
    image = lax.axis_index("dp") // (N_DP // 2)
    residual = jnp.where(image == 0, image_ref[0:1, :], image_ref[1:2, :])
    grad = residual + norm_back(total_ref[...], unit_rows, inverse, gain)
    mine[...] = grad.astype(bf16)
    gather = Gather(RETURN_PLAN, buf, own_send, own_recv)
    copies = []
    for c in range(gather.count):
        copy = pltpu.make_async_remote_copy(
            src_ref=mine.at[:, gather.columns(c)],
            dst_ref=came.at[:, gather.columns(c)],
            send_sem=step_send.at[c],
            recv_sem=step_recv.at[c],
            device_id=section_at(-1),
            device_id_type=MESH,
        )
        copy.start()
        copies.append(copy)
    for load in later:
        load.wait()
    last = lax.axis_index("section") == lax.axis_size("section") - 1

    def take_hop(c):
        copies[c].wait_recv()
        block = came[:, gather.columns(c)]
        buf[rows_of(0, 0), gather.columns(c)] = jnp.where(last, jnp.zeros_like(block), block)

    sums_t = sums_ref[...].T
    hi = sums_t.astype(bf16)
    low = (sums_t - hi.astype(f32)).astype(bf16)
    stores = []

    def margin_piece(k):
        def tile(r, carry):
            part_rows = pl.ds(pl.multiple_of(k * TALL + r * 256, 256), 256)
            margin_part[part_rows, :] = dot_nn(
                margin_turned[part_rows, :], grad_ref[...]
            ).astype(bf16)
            return carry

        lax.fori_loop(0, TALL // 256, tile, 0)
        rows = pl.ds(k * TALL, TALL)
        store = pltpu.make_async_copy(
            margin_part.at[rows, :], margin_part_hbm.at[rows, :], part_sem.at[k]
        )
        store.start()
        stores.append(store)

    def chunk(c, r, first):
        cols = gather.columns(c)
        rows = pl.ds(r * PATCHES, PATCHES)
        value = dot_nt(buf[rows, cols], wout[:, cols])
        if first:
            grad_att_ref[rows, :] = value
        else:
            grad_att_ref[rows, :] += value
        if r == 0:
            return
        shared = image_ref[:, cols].astype(bf16)
        value = dot_nn(turned[...], buf[:, cols])
        value = value + dot_nn(hi, shared) + dot_nn(low, shared)
        grad_out[:, cols] = value.astype(bf16)
        store = pltpu.make_async_copy(
            grad_out.at[:, cols], grad_out_hbm.at[:, cols], out_sem.at[c]
        )
        store.start()
        stores.append(store)

    def side(i):
        if i < 2:
            keep_image(proj, pair_ref, kept, i)
        else:
            margin_piece(i - 2)

    gather.run(RETURN_STEPS, chunk, side, take_hop)

    def cotangent(i, rows, h):
        return grad_att_ref[rows, pl.ds(h * HS, HS)].astype(bf16)

    both_images(lambda i: back_image(kept, pair_ref, cotangent, own_grad_ref, i))
    scatter.finish()
    gather.finish()
    for copy in copies:
        copy.wait_send()
    for store in stores:
        store.wait()


def back(
    grad,
    rows,
    gain_row,
    gain_pair,
    grad_image,
    sums,
    qkv_local,
    out_local,
    turned,
    margin_turned,
    projected,
    collective_id,
):
    return pl.pallas_call(
        back_kernel,
        out_shape=(
            jax.ShapeDtypeStruct((TOTAL, 3 * F), bf16),
            jax.ShapeDtypeStruct((F, D), bf16),
            jax.ShapeDtypeStruct((D, 3 * F), bf16),
        ),
        in_specs=[VM] * 6 + [ANY] * 5,
        out_specs=(VM, ANY, ANY),
        scratch_shapes=land_scratch()
        + [
            pltpu.VMEM((D, 3 * F), bf16),
            pltpu.VMEM((F, D), bf16),
            pltpu.VMEM((F, TOTAL), bf16),
            pltpu.VMEM((D, TOTAL), bf16),
            pltpu.VMEM((ROWS, D), f32),
            pltpu.VMEM((ROWS, D), bf16),
            pltpu.VMEM((ROWS, D), bf16),
            pltpu.VMEM((TOTAL, D), bf16),
            pltpu.VMEM((F, D), bf16),
            pltpu.VMEM((D, 3 * F), bf16),
            pltpu.VMEM((TOTAL, 3 * F), f32),
            pltpu.VMEM((TOTAL, F), f32),
        ]
        + keep_scratch()
        + [
            pltpu.SemaphoreType.DMA((3 * len(INPUT_PLAN),)),
            pltpu.SemaphoreType.DMA((4,)),
            pltpu.SemaphoreType.DMA((len(RETURN_PLAN),)),
            pltpu.SemaphoreType.DMA((STEPS,)),
        ]
        + ring_sems(INPUT_PLAN)
        + [pltpu.SemaphoreType.DMA((len(RETURN_PLAN),))] * 2
        + ring_sems(RETURN_PLAN),
        compiler_params=params(collective_id),
        name="back",
    )(
        grad,
        rows,
        gain_row,
        gain_pair,
        grad_image,
        sums,
        qkv_local,
        out_local,
        turned,
        margin_turned,
        projected,
    )


def finish_kernel(
    grad_ref,
    turned_hbm,
    part_hbm,
    out_in,
    grad_out_in,
    head_in,
    grad_hbm,
    out_hbm,
    grad_out_hbm,
    head_hbm,
    turned,
    part,
    result,
    passed_out,
    passed_grad,
    passed_head,
    load_sem,
    part_sem,
    store_sem,
    pass_sem,
):
    passes = [
        (out_in, passed_out, out_hbm),
        (grad_out_in, passed_grad, grad_out_hbm),
        (head_in, passed_head, head_hbm),
    ]
    def tall_rows(r):
        return pl.ds(pl.multiple_of(r * TALL, TALL), TALL)

    def load_pair(r):
        rows = tall_rows(r)
        return (
            pltpu.make_async_copy(turned_hbm.at[rows, :], turned.at[rows, :], load_sem.at[r]),
            pltpu.make_async_copy(part_hbm.at[rows, :], part.at[rows, :], part_sem.at[r]),
        )

    def store(r):
        rows = tall_rows(r)
        return pltpu.make_async_copy(
            result.at[:, rows, :], grad_hbm.at[:, rows, :], store_sem.at[r]
        )

    for r in range(STEPS):
        for load in load_pair(r):
            load.start()
    through = []
    for k, (source, held, _) in enumerate(passes):
        copy = pltpu.make_async_copy(source, held, pass_sem.at[k])
        copy.start()
        through.append(copy)

    def step(r, carry):
        rows = tall_rows(r)
        for load in load_pair(r):
            load.wait()
        value = dot_nn(turned[rows, :], grad_ref[...]) + part[rows, :].astype(f32)
        for t in range(3):
            result[t, rows, :] = value[:, t * F : (t + 1) * F].astype(bf16)
        store(r).start()
        return carry

    lax.fori_loop(0, STEPS // 2, step, 0)
    stores = []
    for k, (_, held, target) in enumerate(passes):
        through[k].wait()
        copy = pltpu.make_async_copy(held, target, pass_sem.at[k])
        copy.start()
        stores.append(copy)
    lax.fori_loop(STEPS // 2, STEPS, step, 0)
    for copy in stores:
        copy.wait()
    for r in range(STEPS):
        store(r).wait()


def finish(grad, turned, margin_part, out_own, grad_out, grad_head):
    return pl.pallas_call(
        finish_kernel,
        out_shape=(
            jax.ShapeDtypeStruct((3, D, F), bf16),
            jax.ShapeDtypeStruct((ROWS, D), bf16),
            jax.ShapeDtypeStruct((F, D), bf16),
            jax.ShapeDtypeStruct((F, CLASSES), bf16),
        ),
        in_specs=[VM] + [ANY] * 5,
        out_specs=(ANY,) * 4,
        scratch_shapes=[
            pltpu.VMEM((D, TOTAL), bf16),
            pltpu.VMEM((D, 3 * F), bf16),
            pltpu.VMEM((3, D, F), bf16),
            pltpu.VMEM((ROWS, D), bf16),
            pltpu.VMEM((F, D), bf16),
            pltpu.VMEM((F, CLASSES), bf16),
            pltpu.SemaphoreType.DMA((STEPS,)),
            pltpu.SemaphoreType.DMA((STEPS,)),
            pltpu.SemaphoreType.DMA((STEPS,)),
            pltpu.SemaphoreType.DMA((3,)),
        ],
        compiler_params=params(),
        name="finish",
    )(grad, turned, margin_part, out_own, grad_out, grad_head)


def on_device(
    block_inputs, qkv_weights, out_weights, norm_gain, query_key_gain, pool_gain, class_head, labels
):
    rows_in, qkv_local, out_local = block_inputs[0], qkv_weights[0], out_weights[0]
    gain_pair = query_key_gain[0]
    (
        out_own,
        margin_rows,
        projected,
        turned,
        attention_turned,
        margin_turned,
        margin_grad,
        grad_head,
        grad_image,
        sums,
        losses,
    ) = front(
        rows_in, norm_gain, gain_pair, pool_gain, labels, qkv_local, out_local, class_head[0], 0
    )
    own_grad, grad_out, margin_part = back(
        margin_grad,
        margin_rows,
        norm_gain,
        gain_pair,
        grad_image,
        sums,
        qkv_local,
        out_local,
        attention_turned,
        margin_turned,
        projected,
        1,
    )
    qkv_grad, out_own, grad_out, grad_head = finish(
        own_grad, turned, margin_part, out_own, grad_out, grad_head
    )
    return (out_own[None], qkv_grad[None], grad_out[None], grad_head[None], losses)


def solution(mesh):
    in_specs = (
        P("section", ("dp", "tensor"), None),
        P("section", None, None, ("dp", "tensor")),
        P("section", ("dp", "tensor"), None),
        P("section", None),
        P("section", None, None),
        P("section", None),
        P("section", None, None),
        P("section", None),
    )
    out_specs = (
        P("section", ("dp", "tensor"), None),
        P("section", None, None, ("dp", "tensor")),
        P("section", ("dp", "tensor"), None),
        P("section", ("dp", "tensor"), None),
        P("section", None),
    )
    return jax.shard_map(
        on_device, mesh=mesh, in_specs=in_specs, out_specs=out_specs, check_vma=False
    )
```

time: 218 us -> 185 us (0.85)
  Pallas kernels: 215 us -> 183 us
    pallas_call x1, Pallas kernels: 120 us -> 102 us  [front(): pl.pallas_call(front_kernel, out_shape=(jax.ShapeDtypeStruct((ROWS, D), b...]
    pallas_call x3 -> x2, Pallas kernels: 95.7 us -> 80.4 us  [the longest x1 69.2 us: back(): pl.pallas_call(back_kernel, out_shape=(jax.ShapeDtypeStruct((TOTAL, 3 * F...]
where the time goes in v2:
time: 185 us; the launch traced here: 184 us
  Pallas kernels  183 us (99%)
    pallas_call x1, Pallas kernels, front(): pl.pallas_call(front_kernel, out_shape=(jax.ShapeDtypeStruct((ROWS, D), b...  102 us
    pallas_call x1, Pallas kernels, back(): pl.pallas_call(back_kernel, out_shape=(jax.ShapeDtypeStruct((TOTAL, 3 * F...  69.2 us
    pallas_call x1, Pallas kernels, finish(): pl.pallas_call(finish_kernel, out_shape=(jax.ShapeDtypeStruct((3, D, F),...  11.2 us

profile of v2, /device:TPU:1, one launch (start us, length us, event | category | flops | bytes accessed | tf_op | source)
XLA Modules:
  0.0 183.7 jit_solution(16681353615042160164)
XLA Ops:
  0.6 102.1 %front.1 = (bf16[64,3072]{1,0:T(8,128)(2,1)}, bf16[64,3072]{1,0:T(8,128)(2,1)}, f32[512,1152]{1,0:T(8,128)}, bf16[3072,512]{1,0:T(8,128)(2,1)}, bf16[384,512]{1,...) custom-call(bf16[64,3072]{1,0:T(8,128)(2,1)} %bitcast.14, ...), custom_call_target="tpu_custom_call" | custom-call | tf_op jit(solution)/shard_map/front/pallas_call | solution.py:613
  102.8 69.2 %back.1 = (bf16[512,1152]{1,0:T(8,128)(2,1)}, bf16[384,3072]{1,0:T(8,128)(2,1)}, bf16[3072,1152]{1,0:T(8,128)(2,1)}) custom-call(bf16[512,1152]{1,0:T(8,128)(2,1)} %get-tuple-element.23.grad_ref, bf16[64,3072]{1,0:T(8,128)(2,1)} %get-tuple-element.24.rows_ref, f32[1,3072]{1,0:T(1,128)} %gain_ref.3, f32[2,128]{1,0:T(2,128)} %bitcast.16, ...), custom_call_target="tpu_custom_call" | custom-call | tf_op jit(solution)/shard_map/back/pallas_call | solution.py:852
  172.0 0.0 copy-start
  172.0 11.2 %finish.1 = (bf16[3,3072,384]{2,1,0:T(8,128)(2,1)}, bf16[64,3072]{1,0:T(8,128)(2,1)}, bf16[384,3072]{1,0:T(8,128)(2,1)}, bf16[384,512]{1,0:T(8,128)(2,1)}) custom-call(bf16[512,1152]{1,0:T(8,128)(2,1)} %get-tuple-element.30.grad_ref, bf16[3072,512]{1,0:T(8,128)(2,1)} %get-tuple-element.31.turned_hbm, bf16[3072,1152]{1,0:T(8,128)(2,1)} %get-tuple-element.32.part_hbm, ...), custom_call_target="tpu_custom_call" | custom-call | tf_op jit(solution)/shard_map/finish/pallas_call | solution.py:980
  183.2 0.0 copy-done
  183.2 0.5 copy.14
Async XLA Ops:
  172.0 11.2 %copy-start = (f32[1,2]{1,0:T(1,128)S(1)}, f32[1,2]{1,0:T(1,128)}, u32[]{:S(2)}) copy-start(f32[1,2]{1,0:T(1,128)} %get-tuple-element.50) | copy-start | bytes 28

commit v3 on v2

--- a/solution.py
+++ b/solution.py
@@ -401,7 +401,7 @@
 PACK = D // 4
 
 
-def front_kernel(
+def chain_kernel(
     rows_ref,
     gain_ref,
     pair_ref,
@@ -411,21 +411,23 @@
     wout_hbm,
     head_hbm,
     out_ref,
+    turned_hbm,
+    head_grad_ref,
+    loss_ref,
+    own_grad_ref,
+    grad_out_hbm,
+    margin_part_hbm,
     margin_ref,
-    proj_hbm,
-    turned_hbm,
     att_turned_ref,
-    margin_turned_hbm,
     margin_grad_ref,
-    head_grad_ref,
     image_ref,
     sums_ref,
-    loss_ref,
     wbuf,
     wout,
     head,
     buf_own,
     buf_margin,
+    buf,
     proj_own,
     proj_margin,
     turned_own,
@@ -433,28 +435,42 @@
     att,
     part,
     land,
+    back_land,
     next_rows,
     stage,
     pool_land,
     pooled_ref,
     half_ref,
     per_image,
+    total_ref,
+    mine,
+    came,
+    grad_out,
+    grad_att_ref,
+    load_sem,
+    store_sem,
+    step_send,
+    step_recv,
+    pool_send,
+    pool_recv,
+    hop_send,
+    hop_recv,
+    out_sem,
+    part_sem,
     *rest,
 ):
     kept = rest[:5]
     (
-    load_sem,
-    store_sem,
-    own_send,
-    own_recv,
-    sum_send,
-    sum_recv,
-    step_send,
-    step_recv,
-    margin_send,
-    margin_recv,
-    pool_send,
-    pool_recv,
+        own_send,
+        own_recv,
+        sum_send,
+        sum_recv,
+        margin_send,
+        margin_recv,
+        back_send,
+        back_recv,
+        return_send,
+        return_recv,
     ) = rest[5:]
     load_w = side_by_side(w_hbm, wbuf, load_sem)
     load_out = pltpu.make_async_copy(wout_hbm, wout, load_sem.at[3])
@@ -480,8 +496,7 @@
 
     gather.run(PROJECT_STEPS, compute_own)
     stores = [
-        pltpu.make_async_copy(proj_own, proj_hbm, store_sem.at[0]),
-        pltpu.make_async_copy(turned_own, turned_hbm, store_sem.at[1]),
+        pltpu.make_async_copy(turned_own, turned_hbm, store_sem.at[0]),
     ]
     for store in stores:
         store.start()
@@ -530,9 +545,6 @@
             buf_margin, wbuf, proj_margin, turned_margin, first, second.columns(c), r
         ),
     )
-    store = pltpu.make_async_copy(turned_margin, margin_turned_hbm, store_sem.at[2])
-    store.start()
-    stores.append(store)
     sums_ref[...] = jnp.zeros_like(sums_ref)
     both_images(lambda i: keep_image(proj_margin, pair_ref, kept, i, sums_ref))
 
@@ -591,8 +603,8 @@
     z, t = place()
     width = D // (N_DP * N_T)
     start = pl.multiple_of((z * N_T + t) * width, width)
-    mine = half_ref[:, pl.ds(start, width)]
-    head_grad_ref[...] = dot_nn(mine.T.astype(bf16), grad_logits).astype(bf16)
+    pooled_slice = half_ref[:, pl.ds(start, width)]
+    head_grad_ref[...] = dot_nn(pooled_slice.T.astype(bf16), grad_logits).astype(bf16)
 
     def shared_cotangent(i, rows, h):
         cols = pl.ds(h * HS, HS)
@@ -608,136 +620,13 @@
     for store in stores:
         store.wait()
 
-
-def front(rows, gain_row, gain_pair, pool_row, labels, qkv_local, out_local, head_local, collective_id):
-    return pl.pallas_call(
-        front_kernel,
-        out_shape=(
-            jax.ShapeDtypeStruct((ROWS, D), bf16),
-            jax.ShapeDtypeStruct((ROWS, D), bf16),
-            jax.ShapeDtypeStruct((TOTAL, 3 * F), f32),
-            jax.ShapeDtypeStruct((D, TOTAL), bf16),
-            jax.ShapeDtypeStruct((F, TOTAL), bf16),
-            jax.ShapeDtypeStruct((D, TOTAL), bf16),
-            jax.ShapeDtypeStruct((TOTAL, 3 * F), bf16),
-            jax.ShapeDtypeStruct((F, CLASSES), bf16),
-            jax.ShapeDtypeStruct((8, D), f32),
-            jax.ShapeDtypeStruct((8, F), f32),
-            jax.ShapeDtypeStruct((1, 2), f32),
-        ),
-        in_specs=[VM, VM, VM, VM, VM, ANY, ANY, ANY],
-        out_specs=(VM, VM, ANY, ANY, VM, ANY, VM, VM, VM, VM, VM),
-        scratch_shapes=[
-            pltpu.VMEM((D, 3 * F), bf16),
-            pltpu.VMEM((F, D), bf16),
-            pltpu.VMEM((D, CLASSES), bf16),
-            pltpu.VMEM((TOTAL, D), bf16),
-            pltpu.VMEM((TOTAL, D), bf16),
-            pltpu.VMEM((TOTAL, 3 * F), f32),
-            pltpu.VMEM((TOTAL, 3 * F), f32),
-            pltpu.VMEM((D, TOTAL), bf16),
-            pltpu.VMEM((D, TOTAL), bf16),
-            pltpu.VMEM((TOTAL, F), bf16),
-        ]
-        + land_scratch()
-        + [
-            pltpu.VMEM((ROWS, D), bf16),
-            pltpu.VMEM((8, PACK), f32),
-            pltpu.VMEM((len(PEERS), 8, PACK), f32),
-            pltpu.VMEM((8, D), f32),
-            pltpu.VMEM((8, D), f32),
-            pltpu.VMEM((8, F), f32),
-        ]
-        + keep_scratch()
-        + [
-            pltpu.SemaphoreType.DMA((5,)),
-            pltpu.SemaphoreType.DMA((3,)),
-        ]
-        + ring_sems(PROJECT_PLAN)
-        + ring_sems(OUT_PLAN)
-        + [pltpu.SemaphoreType.DMA((len(OUT_PLAN),))] * 2
-        + ring_sems(PROJECT_PLAN)
-        + [pltpu.SemaphoreType.DMA((len(PEERS),)), pltpu.SemaphoreType.DMA((len(PEERS),))],
-        compiler_params=params(collective_id),
-        name="front",
-    )(rows, gain_row, gain_pair, pool_row, labels, qkv_local, out_local, head_local)
-
-
-def back_kernel(
-    grad_ref,
-    rows_ref,
-    gain_ref,
-    pair_ref,
-    image_ref,
-    sums_ref,
-    w_hbm,
-    wout_hbm,
-    turned_hbm,
-    margin_turned_hbm,
-    proj_hbm,
-    own_grad_ref,
-    grad_out_hbm,
-    margin_part_hbm,
-    part,
-    land,
-    wbuf,
-    wout,
-    turned,
-    margin_turned,
-    total_ref,
-    mine,
-    came,
-    buf,
-    grad_out,
-    margin_part,
-    proj,
-    grad_att_ref,
-    *rest,
-):
-    kept = rest[:5]
-    (
-    wsem,
-    load_sem,
-    out_sem,
-    part_sem,
-    sum_send,
-    sum_recv,
-    step_send,
-    step_recv,
-    own_send,
-    own_recv,
-    ) = rest[5:]
-    devices = [neighbour(*way) for way in RING] + [section_at(1), section_at(-1)]
-    greet(devices)
-    scatter = Scatter(INPUT_PLAN, part, land, sum_send, sum_recv)
-    loads = []
-    for c in range(scatter.count):
-        for t in range(3):
-            load = pltpu.make_async_copy(
-                w_hbm.at[t, scatter.columns(c), :],
-                wbuf.at[scatter.columns(c), pl.ds(t * F, F)],
-                wsem.at[3 * c + t],
-            )
-            load.start()
-            loads.append(load)
-    later = [
-        pltpu.make_async_copy(margin_turned_hbm, margin_turned, load_sem.at[0]),
-        pltpu.make_async_copy(wout_hbm, wout, load_sem.at[1]),
-        pltpu.make_async_copy(turned_hbm, turned, load_sem.at[2]),
-        pltpu.make_async_copy(proj_hbm, proj, load_sem.at[3]),
-    ]
-    for load in later:
-        load.start()
-    enter(devices)
-
+    scatter = Scatter(INPUT_PLAN, part, back_land, back_send, back_recv)
     def compute(c):
-        for load in loads[3 * c : 3 * c + 3]:
-            load.wait()
         cols = scatter.columns(c)
 
         def tile(r, carry):
             rows = image_rows(r)
-            part[rows, cols] = dot_nt(grad_ref[rows, :], wbuf[cols, :]).astype(bf16)
+            part[rows, cols] = dot_nt(margin_grad_ref[rows, :], wbuf[cols, :]).astype(bf16)
             return carry
 
         lax.fori_loop(0, TOTAL // PATCHES, tile, 0)
@@ -747,26 +636,24 @@
 
     scatter.run(INPUT_STEPS, compute, done)
     gain = gain_ref[...]
-    _, unit_rows, inverse = norm_last(rows_ref[...].astype(f32), gain)
+    _, unit_rows, inverse = norm_last(margin_ref[...].astype(f32), gain)
     image = lax.axis_index("dp") // (N_DP // 2)
     residual = jnp.where(image == 0, image_ref[0:1, :], image_ref[1:2, :])
     grad = residual + norm_back(total_ref[...], unit_rows, inverse, gain)
     mine[...] = grad.astype(bf16)
-    gather = Gather(RETURN_PLAN, buf, own_send, own_recv)
+    gather = Gather(RETURN_PLAN, buf, return_send, return_recv)
     copies = []
     for c in range(gather.count):
         copy = pltpu.make_async_remote_copy(
             src_ref=mine.at[:, gather.columns(c)],
             dst_ref=came.at[:, gather.columns(c)],
-            send_sem=step_send.at[c],
-            recv_sem=step_recv.at[c],
+            send_sem=hop_send.at[c],
+            recv_sem=hop_recv.at[c],
             device_id=section_at(-1),
             device_id_type=MESH,
         )
         copy.start()
         copies.append(copy)
-    for load in later:
-        load.wait()
     last = lax.axis_index("section") == lax.axis_size("section") - 1
 
     def take_hop(c):
@@ -782,15 +669,15 @@
     def margin_piece(k):
         def tile(r, carry):
             part_rows = pl.ds(pl.multiple_of(k * TALL + r * 256, 256), 256)
-            margin_part[part_rows, :] = dot_nn(
-                margin_turned[part_rows, :], grad_ref[...]
+            wbuf[part_rows, :] = dot_nn(
+                turned_margin[part_rows, :], margin_grad_ref[...]
             ).astype(bf16)
             return carry
 
         lax.fori_loop(0, TALL // 256, tile, 0)
         rows = pl.ds(k * TALL, TALL)
         store = pltpu.make_async_copy(
-            margin_part.at[rows, :], margin_part_hbm.at[rows, :], part_sem.at[k]
+            wbuf.at[rows, :], margin_part_hbm.at[rows, :], part_sem.at[k]
         )
         store.start()
         stores.append(store)
@@ -806,7 +693,7 @@
         if r == 0:
             return
         shared = image_ref[:, cols].astype(bf16)
-        value = dot_nn(turned[...], buf[:, cols])
+        value = dot_nn(att_turned_ref[...], buf[:, cols])
         value = value + dot_nn(hi, shared) + dot_nn(low, shared)
         grad_out[:, cols] = value.astype(bf16)
         store = pltpu.make_async_copy(
@@ -817,7 +704,7 @@
 
     def side(i):
         if i < 2:
-            keep_image(proj, pair_ref, kept, i)
+            keep_image(proj_own, pair_ref, kept, i)
         else:
             margin_piece(i - 2)
 
@@ -835,69 +722,71 @@
         store.wait()
 
 
-def back(
-    grad,
-    rows,
-    gain_row,
-    gain_pair,
-    grad_image,
-    sums,
-    qkv_local,
-    out_local,
-    turned,
-    margin_turned,
-    projected,
-    collective_id,
-):
+def chain(rows, gain_row, gain_pair, pool_row, labels, qkv_local, out_local, head_local):
     return pl.pallas_call(
-        back_kernel,
+        chain_kernel,
         out_shape=(
+            jax.ShapeDtypeStruct((ROWS, D), bf16),
+            jax.ShapeDtypeStruct((D, TOTAL), bf16),
+            jax.ShapeDtypeStruct((F, CLASSES), bf16),
+            jax.ShapeDtypeStruct((1, 2), f32),
             jax.ShapeDtypeStruct((TOTAL, 3 * F), bf16),
             jax.ShapeDtypeStruct((F, D), bf16),
             jax.ShapeDtypeStruct((D, 3 * F), bf16),
         ),
-        in_specs=[VM] * 6 + [ANY] * 5,
-        out_specs=(VM, ANY, ANY),
-        scratch_shapes=land_scratch()
-        + [
+        in_specs=[VM] * 5 + [ANY] * 3,
+        out_specs=(VM, ANY, VM, VM, VM, ANY, ANY),
+        scratch_shapes=[
+            pltpu.VMEM((ROWS, D), bf16),
+            pltpu.VMEM((F, TOTAL), bf16),
+            pltpu.VMEM((TOTAL, 3 * F), bf16),
+            pltpu.VMEM((8, D), f32),
+            pltpu.VMEM((8, F), f32),
             pltpu.VMEM((D, 3 * F), bf16),
             pltpu.VMEM((F, D), bf16),
-            pltpu.VMEM((F, TOTAL), bf16),
+            pltpu.VMEM((D, CLASSES), bf16),
+            pltpu.VMEM((TOTAL, D), bf16),
+            pltpu.VMEM((TOTAL, D), bf16),
+            pltpu.VMEM((TOTAL, D), bf16),
+            pltpu.VMEM((TOTAL, 3 * F), f32),
+            pltpu.VMEM((TOTAL, 3 * F), f32),
             pltpu.VMEM((D, TOTAL), bf16),
+            pltpu.VMEM((D, TOTAL), bf16),
+            pltpu.VMEM((TOTAL, F), bf16),
+            pltpu.VMEM((TOTAL, D), bf16),
+            pltpu.VMEM((7, ROWS, D), bf16),
+            pltpu.VMEM((7, ROWS, D), bf16),
+            pltpu.VMEM((ROWS, D), bf16),
+            pltpu.VMEM((8, PACK), f32),
+            pltpu.VMEM((len(PEERS), 8, PACK), f32),
+            pltpu.VMEM((8, D), f32),
+            pltpu.VMEM((8, D), f32),
+            pltpu.VMEM((8, F), f32),
             pltpu.VMEM((ROWS, D), f32),
             pltpu.VMEM((ROWS, D), bf16),
             pltpu.VMEM((ROWS, D), bf16),
-            pltpu.VMEM((TOTAL, D), bf16),
             pltpu.VMEM((F, D), bf16),
-            pltpu.VMEM((D, 3 * F), bf16),
-            pltpu.VMEM((TOTAL, 3 * F), f32),
             pltpu.VMEM((TOTAL, F), f32),
-        ]
-        + keep_scratch()
-        + [
-            pltpu.SemaphoreType.DMA((3 * len(INPUT_PLAN),)),
-            pltpu.SemaphoreType.DMA((4,)),
+            pltpu.SemaphoreType.DMA((5,)),
+            pltpu.SemaphoreType.DMA((1,)),
+            pltpu.SemaphoreType.DMA((len(OUT_PLAN),)),
+            pltpu.SemaphoreType.DMA((len(OUT_PLAN),)),
+            pltpu.SemaphoreType.DMA((len(PEERS),)),
+            pltpu.SemaphoreType.DMA((len(PEERS),)),
+            pltpu.SemaphoreType.DMA((len(RETURN_PLAN),)),
+            pltpu.SemaphoreType.DMA((len(RETURN_PLAN),)),
             pltpu.SemaphoreType.DMA((len(RETURN_PLAN),)),
             pltpu.SemaphoreType.DMA((STEPS,)),
         ]
+        + keep_scratch()
+        + ring_sems(PROJECT_PLAN)
+        + ring_sems(OUT_PLAN)
+        + ring_sems(PROJECT_PLAN)
         + ring_sems(INPUT_PLAN)
-        + [pltpu.SemaphoreType.DMA((len(RETURN_PLAN),))] * 2
         + ring_sems(RETURN_PLAN),
-        compiler_params=params(collective_id),
-        name="back",
-    )(
-        grad,
-        rows,
-        gain_row,
-        gain_pair,
-        grad_image,
-        sums,
-        qkv_local,
-        out_local,
-        turned,
-        margin_turned,
-        projected,
-    )
+        compiler_params=params(0, 63 * 1024 * 1024),
+        name="chain",
+    )(rows, gain_row, gain_pair, pool_row, labels, qkv_local, out_local, head_local)
 
 
 def finish_kernel(
@@ -1009,34 +898,8 @@
 ):
     rows_in, qkv_local, out_local = block_inputs[0], qkv_weights[0], out_weights[0]
     gain_pair = query_key_gain[0]
-    (
-        out_own,
-        margin_rows,
-        projected,
-        turned,
-        attention_turned,
-        margin_turned,
-        margin_grad,
-        grad_head,
-        grad_image,
-        sums,
-        losses,
-    ) = front(
-        rows_in, norm_gain, gain_pair, pool_gain, labels, qkv_local, out_local, class_head[0], 0
-    )
-    own_grad, grad_out, margin_part = back(
-        margin_grad,
-        margin_rows,
-        norm_gain,
-        gain_pair,
-        grad_image,
-        sums,
-        qkv_local,
-        out_local,
-        attention_turned,
-        margin_turned,
-        projected,
-        1,
+    out_own, turned, grad_head, losses, own_grad, grad_out, margin_part = chain(
+        rows_in, norm_gain, gain_pair, pool_gain, labels, qkv_local, out_local, class_head[0]
     )
     qkv_grad, out_own, grad_out, grad_head = finish(
         own_grad, turned, margin_part, out_own, grad_out, grad_head

time: 185 us -> 179 us (0.968)
  Pallas kernels: 183 us -> 178 us
    pallas_call x2 -> x1, Pallas kernels: 171 us -> 167 us  [chain(): pl.pallas_call(chain_kernel, out_shape=(jax.ShapeDtypeStruct((ROWS, D), b...]
where the time goes in v3:
time: 179 us
  Pallas kernels  178 us (99%)
    pallas_call x1, Pallas kernels, chain(): pl.pallas_call(chain_kernel, out_shape=(jax.ShapeDtypeStruct((ROWS, D), b...  167 us
    pallas_call x1, Pallas kernels, finish(): pl.pallas_call(finish_kernel, out_shape=(jax.ShapeDtypeStruct((3, D, F),...  11.2 us

profile of v3, /device:TPU:1, one launch (start us, length us, event | category | flops | bytes accessed | tf_op | source)
XLA Modules:
  0.0 179.2 jit_solution(5327831261454023763)
XLA Ops:
  0.6 166.8 %chain.1 = (bf16[64,3072]{1,0:T(8,128)(2,1)}, bf16[3072,512]{1,0:T(8,128)(2,1)}, bf16[384,512]{1,0:T(8,128)(2,1)}, f32[1,2]{1,0:T(1,128)}, bf16[512,1152]{1,0:T(...) custom-call(bf16[64,3072]{1,0:T(8,128)(2,1)} %bitcast.12, f32[1,3072]{1,0:T(1,128)} %gain_ref.1, ...), custom_call_target="tpu_custom_call" | custom-call | tf_op jit(solution)/shard_map/chain/pallas_call | solution.py:726
  167.5 0.0 copy-start
  167.5 11.2 %finish.1 = (bf16[3,3072,384]{2,1,0:T(8,128)(2,1)}, bf16[64,3072]{1,0:T(8,128)(2,1)}, bf16[384,3072]{1,0:T(8,128)(2,1)}, bf16[384,512]{1,0:T(8,128)(2,1)}) custom-call(bf16[512,1152]{1,0:T(8,128)(2,1)} %get-tuple-element.16.grad_ref, bf16[3072,512]{1,0:T(8,128)(2,1)} %get-tuple-element.17.turned_hbm, bf16[3072,1152]{1,0:T(8,128)(2,1)} %get-tuple-element.18.part_hbm, ...), custom_call_target="tpu_custom_call" | custom-call | tf_op jit(solution)/shard_map/finish/pallas_call | solution.py:869
  178.7 0.0 copy-done
  178.7 0.5 copy.14
Async XLA Ops:
  167.5 11.2 %copy-start = (f32[1,2]{1,0:T(1,128)S(1)}, f32[1,2]{1,0:T(1,128)}, u32[]{:S(2)}) copy-start(f32[1,2]{1,0:T(1,128)} %get-tuple-element.36) | copy-start | bytes 28
